TPU v7x, 32 devices: a whole 2x2x4 slice. The times are simulated.
32 devices in a mesh: pair: 8 (over y, x, core), tile: 4 (over z).
Axes of the slice: x: 2, y: 2, z: 4, core: 2. Of those that a mesh axis runs over, the one named last changes fastest.
Arguments:
- fixed: float32 [4096, 512], P('pair', 'tile'), parts along dimension 0, may hold values from -6 to 6
- moving: float32 [4096, 512], P('pair', 'tile'), parts along dimension 0, may hold values from -6 to 6
- offsets: int32 [2, 4096, 512], P(None, ('pair', 'tile')), parts along dimension 1, may hold values from -3 to 3
- fractions: float32 [2, 4096, 512], P(None, ('pair', 'tile')), parts along dimension 1, may hold values from 0 to 1
Outputs:
- warped: float32 [4096, 512], P(('pair', 'tile')), parts along dimension 0
There are 8 independent parts, one for each index of `pair`. A program takes and returns all parts, laid end to end along the dimension named above; each array names one. Nothing has to cross between parts.
All inputs are finite; a program needn't handle non-finite values.
Results may differ from a plain program's by a relative error of at most 0.00002.
Values sent between devices are 32-bit elements; how exact they have to be, the bound alone decides.
No kernel may reach another device: no remote copies, remote signals or barrier semaphores. Data moves between devices by JAX's collectives and lax.ppermute only.
A program may use at most 64 MiB of HBM per device.

v0:
```python
import jax
import jax.numpy as jnp
from jax import lax
from jax.sharding import PartitionSpec as P

RADIUS = 4
REACH = 3


def window_sum(extended):
    row_total = extended.shape[0] - 2 * RADIUS
    column_total = extended.shape[1] - 2 * RADIUS
    rows_summed = extended[0:row_total, :]
    for shift in range(1, 2 * RADIUS + 1):
        rows_summed = rows_summed + extended[shift : shift + row_total, :]
    result = rows_summed[:, 0:column_total]
    for shift in range(1, 2 * RADIUS + 1):
        result = result + rows_summed[:, shift : shift + column_total]
    return result


def similarity(fixed_ext, moving_ext):
    window_count = float((2 * RADIUS + 1) ** 2)
    fixed_sum = window_sum(fixed_ext)
    moving_sum = window_sum(moving_ext)
    fixed_square = window_sum(fixed_ext * fixed_ext)
    moving_square = window_sum(moving_ext * moving_ext)
    cross_sum = window_sum(fixed_ext * moving_ext)
    fixed_var = fixed_square - fixed_sum * fixed_sum / window_count
    moving_var = moving_square - moving_sum * moving_sum / window_count
    covariance = cross_sum - fixed_sum * moving_sum / window_count
    correlation = covariance / jnp.sqrt(fixed_var * moving_var + 0.001)
    return 0.5 * (1.0 + correlation)


def sample_corners(padded, offsets, band_rows, column_total, margin):
    zeros = jnp.zeros((band_rows, column_total), jnp.float32)
    left_rows = []
    right_rows = []
    for row_shift in range(-REACH, REACH + 2):
        slab = padded[margin + row_shift : margin + row_shift + band_rows, :]
        left_pick = zeros
        right_pick = zeros
        for col_shift in range(-REACH, REACH + 1):
            chosen = offsets[1] == col_shift
            start = margin + col_shift
            left_pick = jnp.where(chosen, slab[:, start : start + column_total], left_pick)
            right_pick = jnp.where(
                chosen, slab[:, start + 1 : start + 1 + column_total], right_pick
            )
        left_rows.append(left_pick)
        right_rows.append(right_pick)
    top_left, top_right, bottom_left, bottom_right = (zeros, zeros, zeros, zeros)
    for row_shift in range(-REACH, REACH + 1):
        chosen = offsets[0] == row_shift
        place = row_shift + REACH
        top_left = jnp.where(chosen, left_rows[place], top_left)
        top_right = jnp.where(chosen, right_rows[place], top_right)
        bottom_left = jnp.where(chosen, left_rows[place + 1], bottom_left)
        bottom_right = jnp.where(chosen, right_rows[place + 1], bottom_right)
    return (top_left, top_right, bottom_left, bottom_right)


def on_device(fixed, moving, offsets, fractions):
    margin = REACH + 1
    band_rows = offsets.shape[1]
    column_total = offsets.shape[2]
    depth = max(RADIUS, margin)
    stacked = jnp.stack((fixed, moving))
    extent_rows = stacked.shape[1]
    strip_cols = stacked.shape[2]
    band_count = extent_rows // band_rows
    padded_rows = jnp.pad(stacked, ((0, 0), (depth, depth), (0, 0)))
    upper_rim = padded_rows[:, 0:extent_rows, :].reshape(2, band_count, band_rows, strip_cols)[
        :, :, 0:depth, :
    ]
    middle = stacked.reshape(2, band_count, band_rows, strip_cols)
    lower_rim = padded_rows[:, 2 * depth : extent_rows + 2 * depth, :].reshape(
        2, band_count, band_rows, strip_cols
    )[:, :, band_rows - depth :, :]
    blocks = jnp.concatenate((upper_rim, middle, lower_rim), axis=2)
    received = lax.all_to_all(blocks, "tile", split_axis=1, concat_axis=3, tiled=True)
    deepened = received[:, 0]
    window_rows = deepened
    window_rows = jnp.pad(window_rows, ((0, 0), (0, 0), (RADIUS, RADIUS)))
    confidence = similarity(window_rows[0], window_rows[1])
    moving_rows = deepened[1, depth - margin : depth + band_rows + margin, :]
    padded = jnp.pad(moving_rows, ((0, 0), (margin, margin)))
    top_left, top_right, bottom_left, bottom_right = sample_corners(
        padded, offsets, band_rows, column_total, margin
    )
    row_weight = confidence * fractions[0]
    column_weight = confidence * fractions[1]
    upper = (1.0 - column_weight) * top_left + column_weight * top_right
    lower = (1.0 - column_weight) * bottom_left + column_weight * bottom_right
    return (1.0 - row_weight) * upper + row_weight * lower


def solution(mesh):
    placed = (
        P("pair", "tile"),
        P("pair", "tile"),
        P(None, ("pair", "tile"), None),
        P(None, ("pair", "tile"), None),
    )
    return jax.shard_map(
        on_device, mesh=mesh, in_specs=placed, out_specs=P(("pair", "tile"), None), check_vma=False
    )
```

profile of v0, /device:TPU:0, one launch (start us, length us, event | category | flops | bytes accessed | tf_op | source)
XLA Modules:
  0.0 41.1 jit_solution(8555240907671926075)
XLA Ops:
  0.0 1.1 %select_maximum_fusion = f32[2,520,128]{2,1,0:T(8,128)S(1)} fusion(f32[1,512,128]{2,1,0:T(8,128)} %bitcast.78, f32[1,512,128]{2,1,0:T(8,128)} %bitcast.80), kind=kLoop, calls=%fused_computation.79 | loop fusion | flops 798720 | bytes 1056768 | tf_op jit(solution)/shard_map/stack | solution.py:69
  1.1 0.0 copy-start.5
  1.1 0.0 copy-start.6
  1.1 0.1 fusion.124
  1.2 0.9 %copy-done.5 = f32[512,128]{1,0:T(8,128)S(1)} copy-done((f32[512,128]{1,0:T(8,128)S(1)}, f32[512,128]{1,0:T(8,128)}, u32[]{:S(2)}) %copy-start.5) | copy-done | bytes 262168
  2.0 0.1 copy-done.6
  2.1 0.1 pad_maximum_fusion
  2.2 21.3 %all_to_all.15 = f32[2,4,136,128]{3,2,0,1:T(8,128)S(1)} all-to-all(f32[2,4,136,128]{3,2,0,1:T(8,128)S(1)} %pad_maximum_fusion), channel_id=1, replica_groups=mesh['pair'=8,'tile'=4] {'tile'}, dimensions={1} | all-to-all | bytes 1114112 | tf_op jit(solution)/shard_map/all_to_all | solution.py:82
  23.5 0.3 copy.11
  23.8 1.5 %fusion.123 = (f32[1,1,128,4,128]{2,4,3,1,0:T(8,128)}, f32[1,1,128,4,128]{2,4,3,1,0:T(8,128)S(1)}, f32[1,1,128,4,128]{2,4,3,1,0:T(8,128)}, f32[1,1,128,4,128]{2,...) fusion(f32[2,1,136,4,128]{2,4,3,1,0:T(8,128)S(1)} %bitcast.66), kind=kLoop, calls=%fused_computation.269 | loop fusion | bytes 4194304 | tf_op jit(solution)/shard_map/slice | solution.py:47
  25.3 0.1 copy.20
  25.5 0.2 copy.31
  25.6 0.1 copy.28
  25.8 0.1 copy.14
  25.9 0.1 copy.15
  26.1 0.1 copy.16
  26.2 0.8 %copy-done.4 = f32[1,1,128,4,128]{2,4,3,1,0:T(8,128)S(1)} copy-done((f32[1,1,128,4,128]{2,4,3,1,0:T(8,128)S(1)}, f32[1,1,128,4,128]{2,4,3,1,0:T(8,128)}, u32[]{:S(2)}) %copy-start.4) | copy-done | bytes 262168
  27.0 0.1 copy.17
  27.1 0.8 %copy-done.3 = f32[1,1,128,4,128]{2,4,3,1,0:T(8,128)S(1)} copy-done((f32[1,1,128,4,128]{2,4,3,1,0:T(8,128)S(1)}, f32[1,1,128,4,128]{2,4,3,1,0:T(8,128)}, u32[]{:S(2)}) %copy-start.3) | copy-done | bytes 262168
  28.0 0.8 %copy.18 = f32[128,512]{1,0:T(8,128)} copy(f32[128,512]{0,1:T(8,128)S(1)} %bitcast.71) | data formatting | bytes 524288 | tf_op jit(solution)/shard_map/slice | solution.py:47
  28.8 0.1 copy-done.2
  28.9 0.8 %copy.19 = f32[128,512]{1,0:T(8,128)} copy(f32[128,512]{0,1:T(8,128)S(1)} %bitcast.70) | data formatting | bytes 524288 | tf_op jit(solution)/shard_map/slice | solution.py:47
  29.7 0.3 copy.30
  30.0 0.4 %fusion.23 = (f32[1,136,520]{2,1,0:T(8,128)S(1)}, f32[1,136,520]{2,1,0:T(8,128)S(1)}, f32[1,136,520]{2,1,0:T(8,128)S(1)}) fusion(f32[2,136,512]{2,1,0:T(8,128)S(1)} %copy.30), kind=kLoop, calls=%fused_computation.127 | loop fusion | flops 212160 | bytes 1405696 | tf_op jit(solution)/shard_map/mul | solution.py:28
  30.5 1.9 %fusion.18 = (f32[128,520]{1,0:T(8,128)S(1)}, f32[128,520]{1,0:T(8,128)S(1)}, f32[128,520]{1,0:T(8,128)S(1)}) fusion(f32[2,136,512]{2,1,0:T(8,128)S(1)} %copy.30, f32[1,136,520]{2,1,0:T(8,128)S(1)} %get-tuple-element.15), kind=kLoop, calls=%fused_computation.98 | loop fusion | flops 1597440 | bytes 3751936 | tf_op jit(solution)/shard_map/add | solution.py:15
  32.4 0.0 copy-start.1
  32.5 0.5 %fusion.19 = (f32[128,520]{1,0:T(8,128)S(1)}, f32[128,520]{1,0:T(8,128)S(1)}) fusion(f32[1,136,520]{2,1,0:T(8,128)S(1)} %get-tuple-element.17, f32[1,136,520]{2,1,0:T(8,128)S(1)} %get-tuple-element.16), kind=kLoop, calls=%fused_computation.100 | loop fusion | flops 1064960 | bytes 5324800 | tf_op jit(solution)/shard_map/add | solution.py:15
  32.9 0.4 %copy-done = f32[128,512]{1,0:T(8,128)S(1)} copy-done((f32[128,512]{1,0:T(8,128)S(1)}, f32[128,512]{1,0:T(8,128)}, u32[]{:S(2)}) %copy-start) | copy-done | bytes 262168
  33.4 0.1 copy-done.1
  33.4 0.2 copy-done.7
  33.6 0.2 copy-done.8
  33.8 7.3 %fusion.84 = f32[128,512]{1,0:T(8,128)} fusion(f32[128,512]{1,0:T(8,128)S(1)} %copy.20, f32[136,512]{1,0:T(8,128)S(1)} %copy.31, f32[128,512]{1,0:T(8,128)S(1)} %copy.28, f32[128,512]{1,0:T(8,128)S(1)} %copy.14, f32[128,512]{1,0:T(8,128)S(1)} %copy.15, f32[128,512]{1,0:T(8,128)S(1)} %copy.16, f32[128,512]{1,0:T(8,128)S(1)} %copy.17, ...), kind=kLoop, calls=%fused_computation.188 | loop fusion | flops 14483456 | bytes 15482880 | tf_op jit(solution)/shard_map/add | solution.py:96
  (7 shorter events, 0.1 us)
Async XLA Ops:
  1.1 1.0 %copy-start.5 = (f32[512,128]{1,0:T(8,128)S(1)}, f32[512,128]{1,0:T(8,128)}, u32[]{:S(2)}) copy-start(f32[512,128]{1,0:T(8,128)} %param.5) | copy-start | bytes 786436
  1.1 1.0 %copy-start.6 = (f32[512,128]{1,0:T(8,128)S(1)}, f32[512,128]{1,0:T(8,128)}, u32[]{:S(2)}) copy-start(f32[512,128]{1,0:T(8,128)} %param.4) | copy-start | bytes 786436
  26.0 1.0 %copy-start.4 = (f32[1,1,128,4,128]{2,4,3,1,0:T(8,128)S(1)}, f32[1,1,128,4,128]{2,4,3,1,0:T(8,128)}, u32[]{:S(2)}) copy-start(f32[1,1,128,4,128]{2,4,3,1,0:T(8,128)} %get-tuple-element.8) | copy-start | bytes 786436
  27.0 0.9 %copy-start.3 = (f32[1,1,128,4,128]{2,4,3,1,0:T(8,128)S(1)}, f32[1,1,128,4,128]{2,4,3,1,0:T(8,128)}, u32[]{:S(2)}) copy-start(f32[1,1,128,4,128]{2,4,3,1,0:T(8,128)} %get-tuple-element.7) | copy-start | bytes 786436
  27.9 0.9 %copy-start.2 = (f32[1,1,128,4,128]{2,4,3,1,0:T(8,128)S(1)}, f32[1,1,128,4,128]{2,4,3,1,0:T(8,128)}, u32[]{:S(2)}) copy-start(f32[1,1,128,4,128]{2,4,3,1,0:T(8,128)} %get-tuple-element.5) | copy-start | bytes 786436
  32.4 1.0 %copy-start = (f32[128,512]{1,0:T(8,128)S(1)}, f32[128,512]{1,0:T(8,128)}, u32[]{:S(2)}) copy-start(f32[128,512]{1,0:T(8,128)} %copy.18) | copy-start | bytes 786436
  32.4 1.0 %copy-start.1 = (f32[128,512]{1,0:T(8,128)S(1)}, f32[128,512]{1,0:T(8,128)}, u32[]{:S(2)}) copy-start(f32[128,512]{1,0:T(8,128)} %copy.19) | copy-start | bytes 786436
  32.4 1.2 %copy-start.7 = (f32[2,128,512]{2,1,0:T(8,128)S(1)}, f32[2,128,512]{2,1,0:T(8,128)}, u32[]{:S(2)}) copy-start(f32[2,128,512]{2,1,0:T(8,128)} %param.7) | copy-start | bytes 1572868
  32.4 1.3 %copy-start.8 = (s32[2,128,512]{2,1,0:T(8,128)S(1)}, s32[2,128,512]{2,1,0:T(8,128)}, u32[]{:S(2)}) copy-start(s32[2,128,512]{2,1,0:T(8,128)} %param.6) | copy-start | bytes 1572868
where the time goes:
time: 41.4 us; the launch traced here: 41.1 us
  blocking collectives  21.3 us (51%)
  other arithmetic  11.3 us (27%)
  local copies, waits for them, and re-layouts  8.33 us (20%)
    all_to_all x1, blocking collectives, on_device(): lax.all_to_all(blocks, 'tile', split_axis=1, concat_axis=3, tiled=True)  21.3 us
    add x1, other arithmetic, on_device(): return (1.0 - row_weight) * upper + row_weight * lower  7.3 us
    slice x9, local copies, waits for them, and re-layouts, sample_corners(): slab[:, start:start + column_total]  3.89 us
    unnamed x18, local copies, waits for them, and re-layouts  3.54 us
    add x2, other arithmetic, window_sum(): rows_summed = rows_summed + extended[shift:shift + row_total, :]  2.41 us
    another operation x1, other arithmetic, on_device(): stacked = jnp.stack((fixed, moving))  1.07 us

commit v1 on v0

v1 whole, which is shorter than its diff:
```python
import functools

import jax
import jax.numpy as jnp
from jax import lax
from jax.experimental import pallas as pl
from jax.experimental.pallas import tpu as pltpu
from jax.sharding import PartitionSpec as P

RADIUS = 4
REACH = 3
HALO = max(RADIUS, REACH + 1)
LANES = 128
SUB = 8
F32 = jnp.float32


def hops(n):
    middle = n // 2
    return [middle] + [k for k in range(1, n) if k != middle]


def pack_band(strip, out, band, n, rows):
    top = strip[pl.ds(pl.multiple_of(jnp.maximum(band * rows - SUB, 0), SUB), SUB), :]
    out[0:HALO, :] = jnp.where(band > 0, top, 0.0)[SUB - HALO :, :]
    start = pl.multiple_of(band * rows, SUB)
    out[HALO : HALO + rows, :] = strip[pl.ds(start, rows), :]
    low = strip[pl.ds(pl.multiple_of(jnp.minimum(start + rows, n * rows - SUB), SUB), SUB), :]
    out[HALO + rows :, :] = jnp.where(band < n - 1, low, 0.0)[:HALO, :]


def pack_kernel(n, rows, moving, fixed, *refs):
    outs, (mbuf, fbuf, sem) = refs[: 2 * n], refs[2 * n :]
    me = lax.axis_index("tile")
    copies = [
        pltpu.make_async_copy(moving, mbuf, sem.at[0]),
        pltpu.make_async_copy(fixed, fbuf, sem.at[1]),
    ]
    for copy in copies:
        copy.start()
    for image, buf in enumerate((mbuf, fbuf)):
        copies[image].wait()
        for place, k in enumerate(hops(n) + [0]):
            pack_band(buf, outs[image * n + place], lax.rem(me + k, n), n, rows)


def row_sums(load, g):
    total = load(g * SUB)
    for shift in range(1, 2 * RADIUS + 1):
        total = total + load(g * SUB + shift)
    return total


def column_sums(x):
    size = x.shape[1]
    pairs = x + pltpu.roll(x, size - 1, 1)
    fours = pairs + pltpu.roll(pairs, size - 2, 1)
    return fours + pltpu.roll(fours, 4, 1) + pltpu.roll(x, size - 4, 1)


def pick(values, low, high, top):
    even = jnp.where(high, jnp.where(top, values[6], values[4]), jnp.where(top, values[2], values[0]))
    odd = jnp.where(high, jnp.where(top, values[7], values[5]), jnp.where(top, values[3], values[1]))
    after = jnp.where(high, values[6], jnp.where(top, values[4], values[2]))
    return jnp.where(low, odd, even), jnp.where(low, after, odd)


def moving_kernel(n, rows, width, *refs):
    blocks, offsets, fractions = refs[:n], refs[n], refs[n + 1]
    base, linear, square, msum, mvar = refs[n + 2 : n + 7]
    wide, side, sq, rs, rsq, obuf, fbuf, sem = refs[n + 7 :]
    me = lax.axis_index("tile")
    copies = [
        pltpu.make_async_copy(offsets, obuf, sem.at[0]),
        pltpu.make_async_copy(fractions, fbuf, sem.at[1]),
    ]
    for copy in copies:
        copy.start()
    deep = rows + 2 * HALO
    count = float((2 * RADIUS + 1) ** 2)
    rs[:, width:] = jnp.zeros((rows, LANES), F32)
    rsq[:, width:] = jnp.zeros((rows, LANES), F32)
    wide[n] = jnp.zeros((deep, LANES), F32)
    for place, k in enumerate(hops(n) + [0]):
        block = blocks[place]
        source = lax.rem(me - k + n, n)
        wide[source] = block[...]
        sq[...] = block[...] * block[...]
        at = pl.ds(pl.multiple_of(source * LANES, LANES), LANES)
        for g in range(rows // SUB):
            out_rows = slice(g * SUB, (g + 1) * SUB)
            rs[out_rows, at] = row_sums(lambda y: block[y : y + SUB, :], g)
            rsq[out_rows, at] = row_sums(lambda y: sq[y : y + SUB, :], g)
    for g in range(rows // SUB):
        out_rows = slice(g * SUB, (g + 1) * SUB)
        total = column_sums(rs[out_rows, :])[:, :width]
        squares = column_sums(rsq[out_rows, :])[:, :width]
        msum[out_rows, :] = total
        mvar[out_rows, :] = squares - total * total * (1.0 / count)
    lane_deep = lax.broadcasted_iota(jnp.int32, (deep, LANES), 1)
    for s in range(n):
        side[s] = jnp.where(
            lane_deep < LANES // 2, wide[s + 1], wide[s - 1 if s else n]
        )
    for copy in copies:
        copy.wait()
    lane = lax.broadcasted_iota(jnp.int32, (SUB, LANES), 1)

    def unit(g, s):
        y0 = g * SUB
        at = pl.ds(s * LANES, LANES)
        down = obuf[0, y0 : y0 + SUB, at] + REACH
        left = lane + obuf[1, y0 : y0 + SUB, at]
        right = left + 1
        left_in = (left & (LANES - 1)) == left
        right_in = (right & (LANES - 1)) == right
        left = left & (LANES - 1)
        right = right & (LANES - 1)
        lefts, rights = [], []
        take = functools.partial(jnp.take_along_axis, axis=1, mode="promise_in_bounds")
        for r in range(2 * REACH + 2):
            e = y0 + r + HALO - REACH
            own = wide[s, e : e + SUB, :]
            other = side[s, e : e + SUB, :]
            lefts.append(jnp.where(left_in, take(own, left), take(other, left)))
            rights.append(jnp.where(right_in, take(own, right), take(other, right)))
        low = (down & 1) == 1
        high = down >= 4
        top = (down & 2) == 2
        top_left, bottom_left = pick(lefts, low, high, top)
        top_right, bottom_right = pick(rights, low, high, top)
        rf = fbuf[0, y0 : y0 + SUB, at]
        cf = fbuf[1, y0 : y0 + SUB, at]
        across = top_right - top_left
        base[y0 : y0 + SUB, at] = top_left
        linear[y0 : y0 + SUB, at] = cf * across + rf * (bottom_left - top_left)
        square[y0 : y0 + SUB, at] = (rf * cf) * ((bottom_right - bottom_left) - across)

    for g in range(rows // SUB):
        for s in range(n):
            unit(g, s)


def final_kernel(n, rows, width, *refs):
    fixed, moving = refs[:n], refs[n : 2 * n]
    base, linear, square, msum, mvar, out = refs[2 * n : 2 * n + 6]
    sums, ff, fm, obuf, sem = refs[2 * n + 6 :]
    me = lax.axis_index("tile")
    inv = 1.0 / float((2 * RADIUS + 1) ** 2)
    for which in range(3):
        sums[which, :, width:] = jnp.zeros((rows, LANES), F32)
    for place, k in enumerate(hops(n) + [0]):
        f, m = fixed[place], moving[place]
        source = lax.rem(me - k + n, n)
        ff[...] = f[...] * f[...]
        fm[...] = f[...] * m[...]
        at = pl.ds(pl.multiple_of(source * LANES, LANES), LANES)
        for g in range(rows // SUB):
            out_rows = slice(g * SUB, (g + 1) * SUB)
            for which, ref in enumerate((f, ff, fm)):
                sums[which, out_rows, at] = row_sums(lambda y: ref[y : y + SUB, :], g)
    chunks = 4
    per = rows // chunks
    copies = []
    for chunk in range(chunks):
        for g in range(chunk * per // SUB, (chunk + 1) * per // SUB):
            out_rows = slice(g * SUB, (g + 1) * SUB)
            fsum = column_sums(sums[0, out_rows, :])[:, :width]
            fsq = column_sums(sums[1, out_rows, :])[:, :width]
            cross = column_sums(sums[2, out_rows, :])[:, :width]
            ms = msum[out_rows, :]
            fvar = fsq - fsum * fsum * inv
            cov = cross - fsum * ms * inv
            conf = 0.5 + 0.5 * (cov * lax.rsqrt(fvar * mvar[out_rows, :] + 0.001))
            obuf[out_rows, :] = base[out_rows, :] + conf * (
                linear[out_rows, :] + conf * square[out_rows, :]
            )
        copy = pltpu.make_async_copy(
            obuf.at[pl.ds(chunk * per, per), :], out.at[pl.ds(chunk * per, per), :], sem.at[chunk]
        )
        copy.start()
        copies.append(copy)
    for copy in copies:
        copy.wait()


VMEM = pl.BlockSpec(memory_space=pltpu.VMEM)
ANY = pl.BlockSpec(memory_space=pl.ANY)


def on_device(n, fixed, moving, offsets, fractions):
    rows, width = offsets.shape[1:]
    strip = moving.shape
    deep = rows + 2 * HALO
    band = jax.ShapeDtypeStruct((deep, strip[1]), F32)
    plane = jax.ShapeDtypeStruct((rows, width), F32)
    packed = pl.pallas_call(
        functools.partial(pack_kernel, n, rows),
        out_shape=[band] * (2 * n),
        in_specs=[ANY] * 2,
        out_specs=[VMEM] * (2 * n),
        scratch_shapes=[pltpu.VMEM(strip, F32)] * 2 + [pltpu.SemaphoreType.DMA((2,))],
        name="pack",
    )(moving, fixed)
    order = hops(n)

    def send(blocks):
        got = [
            lax.ppermute(block, "tile", [(i, (i + k) % n) for i in range(n)])
            for block, k in zip(blocks, order)
        ]
        return got + [blocks[-1]]

    moved = send(packed[:n])
    fixes = send(packed[n:])
    parts = pl.pallas_call(
        functools.partial(moving_kernel, n, rows, width),
        out_shape=[plane] * 5,
        in_specs=[VMEM] * n + [ANY] * 2,
        out_specs=[VMEM] * 5,
        scratch_shapes=[
            pltpu.VMEM((n + 1, deep, LANES), F32),
            pltpu.VMEM((n, deep, LANES), F32),
            pltpu.VMEM((deep, LANES), F32),
            pltpu.VMEM((rows, width + LANES), F32),
            pltpu.VMEM((rows, width + LANES), F32),
            pltpu.VMEM(offsets.shape, jnp.int32),
            pltpu.VMEM(fractions.shape, F32),
            pltpu.SemaphoreType.DMA((2,)),
        ],
        cost_estimate=pl.CostEstimate(
            flops=200 * rows * width, bytes_accessed=16 * rows * width, transcendentals=0
        ),
        name="moving_part",
    )(*moved, offsets, fractions)
    return pl.pallas_call(
        functools.partial(final_kernel, n, rows, width),
        out_shape=plane,
        in_specs=[VMEM] * (2 * n + 5),
        out_specs=ANY,
        scratch_shapes=[
            pltpu.VMEM((3, rows, width + LANES), F32),
            pltpu.VMEM((deep, LANES), F32),
            pltpu.VMEM((deep, LANES), F32),
            pltpu.VMEM((rows, width), F32),
            pltpu.SemaphoreType.DMA((4,)),
        ],
        name="final_part",
    )(*fixes, *moved, *parts)


def solution(mesh):
    placed = (
        P("pair", "tile"),
        P("pair", "tile"),
        P(None, ("pair", "tile"), None),
        P(None, ("pair", "tile"), None),
    )
    return jax.shard_map(
        functools.partial(on_device, mesh.shape["tile"]),
        mesh=mesh,
        in_specs=placed,
        out_specs=P(("pair", "tile"), None),
        check_vma=False,
    )
```

time: 41.4 us -> 34 us (0.82)
  blocking collectives: 21.3 us -> 0 us
  Pallas kernels: 0 us -> 20.4 us
  starting transfers between devices: 0 us -> 12 us
  other arithmetic: 11.3 us -> 0 us
  local copies, waits for them, and re-layouts: 8.33 us -> 1.28 us
    all_to_all x1 -> x0, blocking collectives: 21.3 us -> none  [on_device(): lax.all_to_all(blocks, 'tile', split_axis=1, concat_axis=3, tiled=True)]
    pallas_call x0 -> x3, Pallas kernels: none -> 20.4 us  [the longest x1 10.5 us: on_device(): pl.pallas_call(functools.partial(moving_kernel, n, rows, width), out_shap...]
    ppermute x0 -> x6, starting transfers between devices: none -> 12 us  [send(): lax.ppermute(block, 'tile', [(i, (i + k) % n) for i in range(n)])]
    add x3 -> x0, other arithmetic: 9.71 us -> none  [the longest x1 7.3 us: on_device(): return (1.0 - row_weight) * upper + row_weight * lower]
    slice x11 -> x0, local copies, waits for them, and re-layouts: 4 us -> none  [the longest x9 3.89 us: sample_corners(): slab[:, start:start + column_total]]
    unnamed x18 -> x12, local copies, waits for them, and re-layouts: 3.54 us -> 1.28 us
    another operation x1 -> x0, other arithmetic: 1.07 us -> none  [on_device(): stacked = jnp.stack((fixed, moving))]
    squeeze x2 -> x0, local copies, waits for them, and re-layouts: 0.46 us -> none  [the longest x1 0.3 us: on_device(): deepened = received[:, 0]]
  transfers between devices with their start and end apart: 0 -> 6, of which waited for: 0 -> 0; matrix products, arithmetic and copies ran while one was open for 0% -> 0% of each run, Pallas kernels for 0% -> 31%
where the time goes in v1:
time: 34 us; the launch traced here: 33.8 us
  Pallas kernels  20.4 us (60%)
  starting transfers between devices  12 us (35%)
  local copies, waits for them, and re-layouts  1.28 us (4%)
    ppermute x6, starting transfers between devices, send(): lax.ppermute(block, 'tile', [(i, (i + k) % n) for i in range(n)])  12 us
    pallas_call x1, Pallas kernels, on_device(): pl.pallas_call(functools.partial(moving_kernel, n, rows, width), out_shap...  10.5 us
    pallas_call x1, Pallas kernels, on_device(): pl.pallas_call(functools.partial(final_kernel, n, rows, width), out_shape...  8.04 us
    pallas_call x1, Pallas kernels, on_device(): pl.pallas_call(functools.partial(pack_kernel, n, rows), out_shape=[band]...  1.85 us
    unnamed x12, local copies, waits for them, and re-layouts  1.28 us
  transfers between devices with their start and end apart: 6, of which 0 were waited for; matrix products, arithmetic and copies ran while one was open for 0% of the time, Pallas kernels for 31%

profile of v1, /device:TPU:0, one launch (start us, length us, event | category | flops | bytes accessed | tf_op | source)
XLA Modules:
  0.0 33.8 jit_solution(12762147811267997664)
XLA Ops:
  0.0 1.8 %pack.1 = (f32[136,128]{1,0:T(8,128)}, f32[136,128]{1,0:T(8,128)}, f32[136,128]{1,0:T(8,128)}, f32[136,128]{1,0:T(8,128)}, f32[136,128]{1,0:T(8,128)}, /*index=5...) custom-call(f32[512,128]{1,0:T(8,128)} %moving.1, f32[512,128]{1,0:T(8,128)} %fixed.1), custom_call_target="tpu_custom_call" | custom-call | tf_op jit(solution)/shard_map/pack/pallas_call | solution.py:197
  1.9 4.1 %collective-permute-start.3 = (f32[136,128]{1,0:T(8,128)}, f32[136,128]{1,0:T(8,128)S(1)}, u32[]{:S(2)}, u32[]{:S(2)}) collective-permute-start(f32[136,128]{1,0:T(8,128)} %get-tuple-element.22), channel_id=1, source_target_pairs={{0,2},{1,3},{2,0},{3,1},{4,6},{5,7},{6,4},{7,5},{8,10},{9,11},{10,... | collective-permute-start | bytes 208904 | tf_op jit(solution)/shard_map/ppermute | solution.py:209
  6.0 1.6 %collective-permute-start.4 = (f32[136,128]{1,0:T(8,128)}, f32[136,128]{1,0:T(8,128)S(1)}, u32[]{:S(2)}, u32[]{:S(2)}) collective-permute-start(f32[136,128]{1,0:T(8,128)} %get-tuple-element.23), channel_id=1, source_target_pairs={{0,1},{1,2},{2,3},{3,0},{4,5},{5,6},{6,7},{7,4},{8,9},{9,10},{10,1... | collective-permute-start | bytes 208904 | tf_op jit(solution)/shard_map/ppermute | solution.py:209
  7.6 2.2 %collective-permute-start.5 = (f32[136,128]{1,0:T(8,128)}, f32[136,128]{1,0:T(8,128)S(1)}, u32[]{:S(2)}, u32[]{:S(2)}) collective-permute-start(f32[136,128]{1,0:T(8,128)} %get-tuple-element.24), channel_id=1, source_target_pairs={{0,3},{1,0},{2,1},{3,2},{4,7},{5,4},{6,5},{7,6},{8,11},{9,8},{10,9... | collective-permute-start | bytes 208904 | tf_op jit(solution)/shard_map/ppermute | solution.py:209
  9.8 0.0 collective-permute-start
  9.8 0.6 %collective-permute-start.1 = (f32[136,128]{1,0:T(8,128)}, f32[136,128]{1,0:T(8,128)S(1)}, u32[]{:S(2)}, u32[]{:S(2)}) collective-permute-start(f32[136,128]{1,0:T(8,128)} %get-tuple-element.19), channel_id=1, source_target_pairs={{0,1},{1,2},{2,3},{3,0},{4,5},{5,6},{6,7},{7,4},{8,9},{9,10},{10,1... | collective-permute-start | bytes 208904 | tf_op jit(solution)/shard_map/ppermute | solution.py:209
  10.4 0.0 collective-permute-done.3.refs_0_.refs_4_
  10.4 0.0 copy-start
  10.4 3.5 %collective-permute-start.2 = (f32[136,128]{1,0:T(8,128)}, f32[136,128]{1,0:T(8,128)S(1)}, u32[]{:S(2)}, u32[]{:S(2)}) collective-permute-start(f32[136,128]{1,0:T(8,128)} %get-tuple-element.20), channel_id=1, source_target_pairs={{0,3},{1,0},{2,1},{3,2},{4,7},{5,4},{6,5},{7,6},{8,11},{9,8},{10,9... | collective-permute-start | bytes 208904 | tf_op jit(solution)/shard_map/ppermute | solution.py:209
  13.9 0.0 collective-permute-done.4.refs_1_.refs_5_
  13.9 0.0 copy-start.1
  13.9 0.0 collective-permute-done.5.refs_2_.refs_6_
  13.9 0.0 copy-start.2
  13.9 0.0 copy-done
  13.9 0.6 %copy-done.1 = f32[136,128]{1,0:T(8,128)} copy-done((f32[136,128]{1,0:T(8,128)}, f32[136,128]{1,0:T(8,128)S(1)}, u32[]{:S(2)}) %copy-start.1) | copy-done | bytes 69656
  14.5 0.0 copy-done.2
  14.6 10.5 %moving_part.1 = (f32[128,512]{1,0:T(8,128)}, f32[128,512]{1,0:T(8,128)}, f32[128,512]{1,0:T(8,128)}, f32[128,512]{1,0:T(8,128)}, f32[128,512]{1,0:T(8,128)}) custom-call(f32[136,128]{1,0:T(8,128)} %copy-done, f32[136,128]{1,0:T(8,128)} %copy-done.1, f32[136,128]{1,0:T(8,128)} %copy-done.2, f32[136,128]{1,0:T(8,128)} %get-tuple-element.25.refs_3_.refs_7_, ...), custom_call_target="tpu_custom_call" | custom-call | flops 13107200 | bytes 1048576 | tf_op jit(solution)/shard_map/moving_part/pallas_call | solution.py:216
  25.0 0.0 collective-permute-done.refs_0_
  25.0 0.0 copy-start.3
  25.1 0.0 collective-permute-done.1.refs_1_
  25.1 0.0 copy-start.4
  25.1 0.0 collective-permute-done.2.refs_2_
  25.1 0.0 copy-start.5
  25.1 0.6 %copy-done.3 = f32[136,128]{1,0:T(8,128)} copy-done((f32[136,128]{1,0:T(8,128)}, f32[136,128]{1,0:T(8,128)S(1)}, u32[]{:S(2)}) %copy-start.3) | copy-done | bytes 69656
  25.7 0.0 copy-done.4
  25.7 0.0 copy-done.5
  25.7 8.0 %final_part.1 = f32[128,512]{1,0:T(8,128)} custom-call(f32[136,128]{1,0:T(8,128)} %copy-done.3, f32[136,128]{1,0:T(8,128)} %copy-done.4, f32[136,128]{1,0:T(8,128)} %copy-done.5, f32[136,128]{1,0:T(8,128)} %get-tuple-element.21.refs_3_, f32[136,128]{1,0:T(8,128)} %copy-done, f32[136,128]{1,0:T(8,128)} %copy-done.1, f32[136,128]{1,0:T(8,128)} %copy-done.2, ...), custom_call_target="tpu_custom_call" | custom-call | tf_op jit(solution)/shard_map/final_part/pallas_call | solution.py:236
Async XLA Ops:
  1.9 8.5 %collective-permute-start.3 = (f32[136,128]{1,0:T(8,128)}, f32[136,128]{1,0:T(8,128)S(1)}, u32[]{:S(2)}, u32[]{:S(2)}) collective-permute-start(f32[136,128]{1,0:T(8,128)} %get-tuple-element.22), channel_id=1, source_target_pairs={{0,2},{1,3},{2,0},{3,1},{4,6},{5,7},{6,4},{7,5},{8,10},{9,11},{10,... | collective-permute-start | bytes 208904 | tf_op jit(solution)/shard_map/ppermute | solution.py:209
  6.0 7.9 %collective-permute-start.4 = (f32[136,128]{1,0:T(8,128)}, f32[136,128]{1,0:T(8,128)S(1)}, u32[]{:S(2)}, u32[]{:S(2)}) collective-permute-start(f32[136,128]{1,0:T(8,128)} %get-tuple-element.23), channel_id=1, source_target_pairs={{0,1},{1,2},{2,3},{3,0},{4,5},{5,6},{6,7},{7,4},{8,9},{9,10},{10,1... | collective-permute-start | bytes 208904 | tf_op jit(solution)/shard_map/ppermute | solution.py:209
  7.6 6.3 %collective-permute-start.5 = (f32[136,128]{1,0:T(8,128)}, f32[136,128]{1,0:T(8,128)S(1)}, u32[]{:S(2)}, u32[]{:S(2)}) collective-permute-start(f32[136,128]{1,0:T(8,128)} %get-tuple-element.24), channel_id=1, source_target_pairs={{0,3},{1,0},{2,1},{3,2},{4,7},{5,4},{6,5},{7,6},{8,11},{9,8},{10,9... | collective-permute-start | bytes 208904 | tf_op jit(solution)/shard_map/ppermute | solution.py:209
  9.8 15.2 %collective-permute-start = (f32[136,128]{1,0:T(8,128)}, f32[136,128]{1,0:T(8,128)S(1)}, u32[]{:S(2)}, u32[]{:S(2)}) collective-permute-start(f32[136,128]{1,0:T(8,128)} %get-tuple-element.18), channel_id=1, source_target_pairs={{0,2},{1,3},{2,0},{3,1},{4,6},{5,7},{6,4},{7,5},{8,10},{9,11},{10,... | collective-permute-start | bytes 208904 | tf_op jit(solution)/shard_map/ppermute | solution.py:209
  9.8 15.2 %collective-permute-start.1 = (f32[136,128]{1,0:T(8,128)}, f32[136,128]{1,0:T(8,128)S(1)}, u32[]{:S(2)}, u32[]{:S(2)}) collective-permute-start(f32[136,128]{1,0:T(8,128)} %get-tuple-element.19), channel_id=1, source_target_pairs={{0,1},{1,2},{2,3},{3,0},{4,5},{5,6},{6,7},{7,4},{8,9},{9,10},{10,1... | collective-permute-start | bytes 208904 | tf_op jit(solution)/shard_map/ppermute | solution.py:209
  10.4 3.5 %copy-start = (f32[136,128]{1,0:T(8,128)}, f32[136,128]{1,0:T(8,128)S(1)}, u32[]{:S(2)}) copy-start(f32[136,128]{1,0:T(8,128)S(1)} %collective-permute-done.3.refs_0_.refs_4_) | copy-start | bytes 208900
  10.4 14.7 %collective-permute-start.2 = (f32[136,128]{1,0:T(8,128)}, f32[136,128]{1,0:T(8,128)S(1)}, u32[]{:S(2)}, u32[]{:S(2)}) collective-permute-start(f32[136,128]{1,0:T(8,128)} %get-tuple-element.20), channel_id=1, source_target_pairs={{0,3},{1,0},{2,1},{3,2},{4,7},{5,4},{6,5},{7,6},{8,11},{9,8},{10,9... | collective-permute-start | bytes 208904 | tf_op jit(solution)/shard_map/ppermute | solution.py:209
  13.9 0.6 %copy-start.1 = (f32[136,128]{1,0:T(8,128)}, f32[136,128]{1,0:T(8,128)S(1)}, u32[]{:S(2)}) copy-start(f32[136,128]{1,0:T(8,128)S(1)} %collective-permute-done.4.refs_1_.refs_5_) | copy-start | bytes 208900
  13.9 0.6 %copy-start.2 = (f32[136,128]{1,0:T(8,128)}, f32[136,128]{1,0:T(8,128)S(1)}, u32[]{:S(2)}) copy-start(f32[136,128]{1,0:T(8,128)S(1)} %collective-permute-done.5.refs_2_.refs_6_) | copy-start | bytes 208900
  25.0 0.6 %copy-start.3 = (f32[136,128]{1,0:T(8,128)}, f32[136,128]{1,0:T(8,128)S(1)}, u32[]{:S(2)}) copy-start(f32[136,128]{1,0:T(8,128)S(1)} %collective-permute-done.refs_0_) | copy-start | bytes 208900
  25.1 0.6 %copy-start.4 = (f32[136,128]{1,0:T(8,128)}, f32[136,128]{1,0:T(8,128)S(1)}, u32[]{:S(2)}) copy-start(f32[136,128]{1,0:T(8,128)S(1)} %collective-permute-done.1.refs_1_) | copy-start | bytes 208900
  25.1 0.6 %copy-start.5 = (f32[136,128]{1,0:T(8,128)}, f32[136,128]{1,0:T(8,128)S(1)}, u32[]{:S(2)}) copy-start(f32[136,128]{1,0:T(8,128)S(1)} %collective-permute-done.2.refs_2_) | copy-start | bytes 208900

commit v2 on v1

v2 whole, which is shorter than its diff:
```python
import functools

import jax
import jax.numpy as jnp
from jax import lax
from jax.experimental import pallas as pl
from jax.experimental.pallas import tpu as pltpu
from jax.sharding import PartitionSpec as P

RADIUS = 4
REACH = 3
HALO = max(RADIUS, REACH + 1)
LANES = 128
SUB = 8
F32 = jnp.float32
BF16 = jnp.bfloat16
ROOM = 28 * 2**20


def hops(n):
    middle = n // 2
    return [middle] + [k for k in range(1, n) if k != middle]


def pack_band(strip, out, band, n, rows):
    top = strip[pl.ds(pl.multiple_of(jnp.maximum(band * rows - SUB, 0), SUB), SUB), :]
    out[0:HALO, :] = jnp.where(band > 0, top, 0.0)[SUB - HALO :, :]
    start = pl.multiple_of(band * rows, SUB)
    out[HALO : HALO + rows, :] = strip[pl.ds(start, rows), :]
    low = strip[pl.ds(pl.multiple_of(jnp.minimum(start + rows, n * rows - SUB), SUB), SUB), :]
    out[HALO + rows :, :] = jnp.where(band < n - 1, low, 0.0)[:HALO, :]


def pack_kernel(n, rows, moving, fixed, *refs):
    outs, (mbuf, fbuf, sem) = refs[: 2 * n], refs[2 * n :]
    me = lax.axis_index("tile")
    copies = [
        pltpu.make_async_copy(moving, mbuf, sem.at[0]),
        pltpu.make_async_copy(fixed, fbuf, sem.at[1]),
    ]
    for copy in copies:
        copy.start()
    for image, buf in enumerate((mbuf, fbuf)):
        copies[image].wait()
        for place, k in enumerate(hops(n) + [0]):
            pack_band(buf, outs[image * n + place], lax.rem(me + k, n), n, rows)


def row_sums(ref, out, rows):
    for g in range((rows + SUB) // SUB):
        y = g * SUB
        last = min(SUB, rows + 6 - y)
        out[y : y + last, :] = (
            ref[y : y + last, :] + ref[y + 1 : y + 1 + last, :] + ref[y + 2 : y + 2 + last, :]
        )

    def total(y, size):
        return out[y : y + size, :] + out[y + 3 : y + 3 + size, :] + out[y + 6 : y + 6 + size, :]

    return total


def split(x):
    high = x.astype(BF16)
    rest = x - high.astype(F32)
    middle = rest.astype(BF16)
    low = (rest - middle.astype(F32)).astype(BF16)
    return high, middle, low


def put(terms, source, y, x):
    at = pl.ds(pl.multiple_of((source + 1) * LANES, LANES), LANES)
    for t, part in enumerate(split(x)):
        terms[t, y : y + x.shape[0], at] = part


def clear_ends(terms):
    zeros = jnp.zeros((terms.shape[1], LANES), BF16)
    for t in range(3):
        terms[t, :, :LANES] = zeros
        terms[t, :, terms.shape[2] - LANES :] = zeros


def lane_sums(arrays, width, size, weights):
    wide = size + 2 * LANES
    left = [
        jnp.concatenate([terms[t, :, start : start + wide] for t in range(3)], axis=1)
        for terms in arrays
        for start in range(0, width, size)
    ]
    out = jnp.dot(jnp.concatenate(left, axis=0), weights, preferred_element_type=F32)
    rows = arrays[0].shape[1]
    parts = [out[i * rows : (i + 1) * rows] for i in range(len(left))]
    count = width // size
    return [parts[i * count : (i + 1) * count] for i in range(len(arrays))]


def band_matrix(first, last, size):
    shape = (size + 2 * LANES, size)
    source = lax.broadcasted_iota(jnp.int32, shape, 0)
    target = lax.broadcasted_iota(jnp.int32, shape, 1)
    distance = source - target - LANES
    band = jnp.where((distance >= first) & (distance <= last), 1.0, 0.0).astype(BF16)
    return jnp.concatenate([band] * 3, axis=0)


def narrow(values, bit):
    return [jnp.where(bit, values[i + 4], values[i]) for i in range(4)] + [values[4]]


def moving_kernel(n, rows, width, *refs):
    blocks, offsets, fractions = refs[:n], refs[n], refs[n + 1]
    base, linear, square, msum, mvar = refs[n + 2 : n + 7]
    image, sums, squares, shifted, sq, three, obuf, fbuf, sem = refs[n + 7 :]
    me = lax.axis_index("tile")
    copies = [
        pltpu.make_async_copy(offsets, obuf, sem.at[0]),
        pltpu.make_async_copy(fractions, fbuf, sem.at[1]),
    ]
    for copy in copies:
        copy.start()
    deep = rows + 2 * HALO
    inv = 1.0 / float((2 * RADIUS + 1) ** 2)
    for terms in (sums, squares):
        clear_ends(terms)
    for place, k in enumerate(hops(n) + [0]):
        block = blocks[place]
        source = lax.rem(me - k + n, n)
        for y in range(0, deep, 2 * SUB):
            size = min(2 * SUB, deep - y)
            x = block[y : y + size, :]
            sq[place, y : y + size, :] = x * x
            at = pl.ds(pl.multiple_of(source * LANES, LANES), LANES)
            image[y : y + size, at] = x
        for which, (ref, terms) in enumerate(((block, sums), (sq.at[place], squares))):
            total = row_sums(ref, three.at[which, place], rows)
            for y in range(0, rows, 2 * SUB):
                put(terms, source, y, total(y, 2 * SUB))
    size = LANES * (2 if n % 2 == 0 else 1)
    window = band_matrix(-RADIUS, RADIUS, size)
    totals, seconds = lane_sums((sums, squares), width, size, window)
    for place, (total, second) in enumerate(zip(totals, seconds)):
        at = pl.ds(place * size, size)
        msum[:, at] = total
        mvar[:, at] = second - total * total * inv
    image[:, width:] = jnp.zeros((deep, LANES), F32)
    for y in range(0, deep, SUB):
        x = image[y : y + SUB, :]
        for c in range(-REACH, REACH + 2):
            turned = pltpu.roll(x, (-c) % x.shape[1], 1) if c else x
            for block in range(n):
                shifted[block, c + REACH, y : y + SUB, :] = turned[
                    :, block * LANES : (block + 1) * LANES
                ]
    for copy in copies:
        copy.wait()
    span = 2 * REACH + 2

    def unit(s, y0):
        at = pl.ds(s * LANES, LANES)
        down = obuf[0, y0 : y0 + SUB, at] + REACH
        along = obuf[1, y0 : y0 + SUB, at] + REACH
        down_bits = [down >= 4, (down & 2) == 2, (down & 1) == 1]
        along_bits = [along >= 4, (along & 2) == 2, (along & 1) == 1]

        def load(r):
            e = y0 + r + HALO - REACH
            return [shifted[s, c, e : e + SUB, :] for c in range(span)]

        grid = []
        for r in range(5):
            line = load(r)
            if r < 4:
                line = [jnp.where(down_bits[0], b, a) for a, b in zip(line, load(r + 4))]
            grid.append(narrow(line, along_bits[0]))
        for place, step in ((1, 2), (2, 1)):
            across_bit, down_bit = along_bits[place], down_bits[place]
            lines = [
                [jnp.where(down_bit, b, a) for a, b in zip(grid[r], grid[r + step])]
                for r in range(step + 1)
            ]
            grid = [
                [jnp.where(across_bit, line[i + step], line[i]) for i in range(step + 1)]
                for line in lines
            ]
        (top_left, top_right), (bottom_left, bottom_right) = grid
        rf = fbuf[0, y0 : y0 + SUB, at]
        cf = fbuf[1, y0 : y0 + SUB, at]
        across = top_right - top_left
        base[y0 : y0 + SUB, at] = top_left
        linear[y0 : y0 + SUB, at] = cf * across + rf * (bottom_left - top_left)
        square[y0 : y0 + SUB, at] = (rf * cf) * ((bottom_right - bottom_left) - across)

    for s in range(n):
        for g in range(rows // SUB):
            unit(s, g * SUB)


def final_kernel(n, rows, width, *refs):
    fixed, moving = refs[:n], refs[n : 2 * n]
    base, linear, square, msum, mvar, out = refs[2 * n : 2 * n + 6]
    sums, squares, crosses, ff, fm, three, obuf, sem = refs[2 * n + 6 :]
    me = lax.axis_index("tile")
    inv = 1.0 / float((2 * RADIUS + 1) ** 2)
    for terms in (sums, squares, crosses):
        clear_ends(terms)
    for place, k in enumerate(hops(n) + [0]):
        f, m = fixed[place], moving[place]
        source = lax.rem(me - k + n, n)
        for y in range(0, rows + 2 * HALO, SUB):
            x = f[y : y + SUB, :]
            ff[place, y : y + SUB, :] = x * x
            fm[place, y : y + SUB, :] = x * m[y : y + SUB, :]
        for which, (ref, terms) in enumerate(
            ((f, sums), (ff.at[place], squares), (fm.at[place], crosses))
        ):
            total = row_sums(ref, three.at[which, place], rows)
            for y in range(0, rows, 2 * SUB):
                put(terms, source, y, total(y, 2 * SUB))
    size = LANES * (2 if n % 2 == 0 else 1)
    window = band_matrix(-RADIUS, RADIUS, size)
    copies = []
    windows = lane_sums((sums, squares, crosses), width, size, window)
    for place, (fsum, second, cross) in enumerate(zip(*windows)):
        at = pl.ds(place * size, size)
        fvar = second - fsum * fsum * inv
        cov = cross - fsum * msum[:, at] * inv
        conf = 0.5 + 0.5 * (cov * lax.rsqrt(fvar * mvar[:, at] + 0.001))
        obuf[:, at] = base[:, at] + conf * (linear[:, at] + conf * square[:, at])
        copy = pltpu.make_async_copy(obuf.at[:, at], out.at[:, at], sem.at[place])
        copy.start()
        copies.append(copy)
    for copy in copies:
        copy.wait()


VMEM = pl.BlockSpec(memory_space=pltpu.VMEM)
ANY = pl.BlockSpec(memory_space=pl.ANY)


def held(shape):
    return pltpu.VMEM(shape, F32)


def near(x):
    return pltpu.with_memory_space_constraint(x, pltpu.VMEM)


def on_device(n, fixed, moving, offsets, fractions):
    rows, width = offsets.shape[1:]
    strip = moving.shape
    deep = rows + 2 * HALO
    band = held((deep, strip[1]))
    plane = held((rows, width))
    packed = pl.pallas_call(
        functools.partial(pack_kernel, n, rows),
        out_shape=[band] * (2 * n),
        in_specs=[ANY] * 2,
        out_specs=[VMEM] * (2 * n),
        scratch_shapes=[pltpu.VMEM(strip, F32)] * 2 + [pltpu.SemaphoreType.DMA((2,))],
        compiler_params=pltpu.CompilerParams(vmem_limit_bytes=ROOM),
        name="pack",
    )(moving, fixed)
    order = hops(n)

    def send(blocks):
        got = [
            lax.ppermute(block, "tile", [(i, (i + k) % n) for i in range(n)])
            for block, k in zip(blocks, order)
        ]
        return got + [blocks[-1]]

    moved = send(packed[:n])
    fixes = send(packed[n:])
    parts = pl.pallas_call(
        functools.partial(moving_kernel, n, rows, width),
        out_shape=[plane] * 5,
        in_specs=[VMEM] * n + [ANY] * 2,
        out_specs=[VMEM] * 5,
        scratch_shapes=[
            pltpu.VMEM((deep, width + LANES), F32),
            pltpu.VMEM((3, rows, width + 2 * LANES), BF16),
            pltpu.VMEM((3, rows, width + 2 * LANES), BF16),
            pltpu.VMEM((n, 2 * REACH + 2, deep, LANES), F32),
            pltpu.VMEM((n, deep, LANES), F32),
            pltpu.VMEM((2, n, deep, LANES), F32),
            pltpu.VMEM(offsets.shape, jnp.int32),
            pltpu.VMEM(fractions.shape, F32),
            pltpu.SemaphoreType.DMA((2,)),
        ],
        compiler_params=pltpu.CompilerParams(vmem_limit_bytes=ROOM),
        cost_estimate=pl.CostEstimate(
            flops=200 * rows * width, bytes_accessed=16 * rows * width, transcendentals=0
        ),
        name="moving_part",
    )(*map(near, moved), offsets, fractions)
    return pl.pallas_call(
        functools.partial(final_kernel, n, rows, width),
        out_shape=jax.ShapeDtypeStruct((rows, width), F32),
        in_specs=[VMEM] * (2 * n + 5),
        out_specs=ANY,
        scratch_shapes=[
            pltpu.VMEM((3, rows, width + 2 * LANES), BF16),
            pltpu.VMEM((3, rows, width + 2 * LANES), BF16),
            pltpu.VMEM((3, rows, width + 2 * LANES), BF16),
            pltpu.VMEM((n, deep, LANES), F32),
            pltpu.VMEM((n, deep, LANES), F32),
            pltpu.VMEM((3, n, deep, LANES), F32),
            pltpu.VMEM((rows, width), F32),
            pltpu.SemaphoreType.DMA((n,)),
        ],
        compiler_params=pltpu.CompilerParams(vmem_limit_bytes=ROOM),
        name="final_part",
    )(*map(near, (*fixes, *moved, *parts)))


def solution(mesh):
    placed = (
        P("pair", "tile"),
        P("pair", "tile"),
        P(None, ("pair", "tile"), None),
        P(None, ("pair", "tile"), None),
    )
    return jax.shard_map(
        functools.partial(on_device, mesh.shape["tile"]),
        mesh=mesh,
        in_specs=placed,
        out_specs=P(("pair", "tile"), None),
        check_vma=False,
    )
```

time: 34 us -> 19.8 us (0.58)
  Pallas kernels: 20.4 us -> 4 us
  local copies, waits for them, and re-layouts: 1.28 us -> 2.94 us
  waiting for transfers between devices: 0.02 us -> 0.83 us
    pallas_call x1, Pallas kernels: 10.5 us -> 1.97 us  [on_device(): pl.pallas_call(functools.partial(moving_kernel, n, rows, width), out_shap...]
    pallas_call x1, Pallas kernels: 8.04 us -> 1.93 us  [on_device(): pl.pallas_call(functools.partial(final_kernel, n, rows, width), out_shape...]
    pallas_call x1, Pallas kernels: 1.85 us -> 0.1 us  [on_device(): pl.pallas_call(functools.partial(pack_kernel, n, rows), out_shape=[band]...]
    unnamed x12 -> x8, local copies, waits for them, and re-layouts: 1.28 us -> 2.94 us
    ppermute x6, waiting for transfers between devices: 0.02 us -> 0.83 us  [send(): lax.ppermute(block, 'tile', [(i, (i + k) % n) for i in range(n)])]
  transfers between devices with their start and end apart: 6 -> 6, of which waited for: 0 -> 2; matrix products, arithmetic and copies ran while one was open for 0% -> 0% of each run, Pallas kernels for 31% -> 10%
where the time goes in v2:
time: 19.8 us; the launch traced here: 19.6 us
  starting transfers between devices  11.8 us (60%)
  Pallas kernels  4 us (20%)
  local copies, waits for them, and re-layouts  2.94 us (15%)
  waiting for transfers between devices  0.83 us (4%)
    ppermute x6, starting transfers between devices, send(): lax.ppermute(block, 'tile', [(i, (i + k) % n) for i in range(n)])  11.8 us
    unnamed x8, local copies, waits for them, and re-layouts  2.94 us
    pallas_call x1, Pallas kernels, on_device(): pl.pallas_call(functools.partial(moving_kernel, n, rows, width), out_shap...  1.97 us
    pallas_call x1, Pallas kernels, on_device(): pl.pallas_call(functools.partial(final_kernel, n, rows, width), out_shape...  1.93 us
    ppermute x6, waiting for transfers between devices, send(): lax.ppermute(block, 'tile', [(i, (i + k) % n) for i in range(n)])  0.83 us
  transfers between devices with their start and end apart: 6, of which 2 were waited for; matrix products, arithmetic and copies ran while one was open for 0% of the time, Pallas kernels for 10%

profile of v2, /device:TPU:0, one launch (start us, length us, event | category | flops | bytes accessed | tf_op | source)
XLA Modules:
  0.0 19.6 jit_solution(10073476554550709825)
XLA Ops:
  0.0 0.0 copy-start.2
  0.0 0.9 %copy-done.2 = f32[512,128]{1,0:T(8,128)S(1)} copy-done((f32[512,128]{1,0:T(8,128)S(1)}, f32[512,128]{1,0:T(8,128)}, u32[]{:S(2)}) %copy-start.2) | copy-done | bytes 262168
  1.0 0.0 copy-start.3
  1.0 0.9 %copy-done.3 = f32[512,128]{1,0:T(8,128)S(1)} copy-done((f32[512,128]{1,0:T(8,128)S(1)}, f32[512,128]{1,0:T(8,128)}, u32[]{:S(2)}) %copy-start.3) | copy-done | bytes 262168
  1.9 0.0 copy-start
  1.9 0.1 pack.1
  2.0 4.1 %collective-permute-start.3 = (f32[136,128]{1,0:T(8,128)S(1)}, f32[136,128]{1,0:T(8,128)S(1)}, u32[]{:S(2)}, u32[]{:S(2)}) collective-permute-start(f32[136,128]{1,0:T(8,128)S(1)} %get-tuple-element.22), channel_id=1, source_target_pairs={{0,2},{1,3},{2,0},{3,1},{4,6},{5,7},{6,4},{7,5},{8,10},{9,11},{10,... | collective-permute-start | bytes 208904 | tf_op jit(solution)/shard_map/ppermute | solution.py:268
  6.1 1.6 %collective-permute-start.4 = (f32[136,128]{1,0:T(8,128)S(1)}, f32[136,128]{1,0:T(8,128)S(1)}, u32[]{:S(2)}, u32[]{:S(2)}) collective-permute-start(f32[136,128]{1,0:T(8,128)S(1)} %get-tuple-element.23), channel_id=1, source_target_pairs={{0,1},{1,2},{2,3},{3,0},{4,5},{5,6},{6,7},{7,4},{8,9},{9,10},{10,1... | collective-permute-start | bytes 208904 | tf_op jit(solution)/shard_map/ppermute | solution.py:268
  7.7 2.2 %collective-permute-start.5 = (f32[136,128]{1,0:T(8,128)S(1)}, f32[136,128]{1,0:T(8,128)S(1)}, u32[]{:S(2)}, u32[]{:S(2)}) collective-permute-start(f32[136,128]{1,0:T(8,128)S(1)} %get-tuple-element.24), channel_id=1, source_target_pairs={{0,3},{1,0},{2,1},{3,2},{4,7},{5,4},{6,5},{7,6},{8,11},{9,8},{10,9... | collective-permute-start | bytes 208904 | tf_op jit(solution)/shard_map/ppermute | solution.py:268
  10.0 0.0 collective-permute-start
  10.0 0.6 %collective-permute-start.1 = (f32[136,128]{1,0:T(8,128)S(1)}, f32[136,128]{1,0:T(8,128)S(1)}, u32[]{:S(2)}, u32[]{:S(2)}) collective-permute-start(f32[136,128]{1,0:T(8,128)S(1)} %get-tuple-element.19), channel_id=1, source_target_pairs={{0,1},{1,2},{2,3},{3,0},{4,5},{5,6},{6,7},{7,4},{8,9},{9,10},{10,1... | collective-permute-start | bytes 208904 | tf_op jit(solution)/shard_map/ppermute | solution.py:268
  10.5 0.0 collective-permute-done.3.refs_0_.refs_4_
  10.5 3.3 %collective-permute-start.2 = (f32[136,128]{1,0:T(8,128)S(1)}, f32[136,128]{1,0:T(8,128)S(1)}, u32[]{:S(2)}, u32[]{:S(2)}) collective-permute-start(f32[136,128]{1,0:T(8,128)S(1)} %get-tuple-element.20), channel_id=1, source_target_pairs={{0,3},{1,0},{2,1},{3,2},{4,7},{5,4},{6,5},{7,6},{8,11},{9,8},{10,9... | collective-permute-start | bytes 208904 | tf_op jit(solution)/shard_map/ppermute | solution.py:268
  13.8 0.0 collective-permute-done.4.refs_1_.refs_5_
  13.8 0.0 collective-permute-done.5.refs_2_.refs_6_
  13.8 0.0 copy-done
  13.8 0.0 copy-start.1
  13.9 1.0 %copy-done.1 = f32[2,128,512]{2,1,0:T(8,128)S(1)} copy-done((f32[2,128,512]{2,1,0:T(8,128)S(1)}, f32[2,128,512]{2,1,0:T(8,128)}, u32[]{:S(2)}) %copy-start.1) | copy-done | bytes 524312
  14.9 2.0 %moving_part.1 = (f32[128,512]{1,0:T(8,128)S(1)}, f32[128,512]{1,0:T(8,128)S(1)}, f32[128,512]{1,0:T(8,128)S(1)}, f32[128,512]{1,0:T(8,128)S(1)}, f32[128,512]{1,0:T(8,128)S(1)}) custom-call(f32[136,128]{1,0:T(8,128)S(1)} %collective-permute-done.3.refs_0_.refs_4_, f32[136,128]{1,0:T(8,128)S(1)} %collective-permute-done.4.refs_1_.refs_5_, ...), custom_call_target="tpu_custom_call" | custom-call | flops 13107200 | bytes 1048576 | tf_op jit(solution)/shard_map/moving_part/pallas_call | solution.py:275
  16.9 0.7 %collective-permute-done.refs_0_ = f32[136,128]{1,0:T(8,128)S(1)} collective-permute-done((f32[136,128]{1,0:T(8,128)S(1)}, f32[136,128]{1,0:T(8,128)S(1)}, u32[]{:S(2)}, u32[]{:S(2)}) %collective-permute-start) | collective-permute-done | bytes 69664 | tf_op jit(solution)/shard_map/ppermute | solution.py:268
  17.6 0.0 collective-permute-done.1.refs_1_
  17.6 0.1 collective-permute-done.2.refs_2_
  17.7 1.9 %final_part.1 = f32[128,512]{1,0:T(8,128)} custom-call(f32[136,128]{1,0:T(8,128)S(1)} %collective-permute-done.refs_0_, f32[136,128]{1,0:T(8,128)S(1)} %collective-permute-done.1.refs_1_, f32[136,128]{1,0:T(8,128)S(1)} %collective-permute-done.2.refs_2_, f32[136,128]{1,0:T(8,128)S(1)} %get-tuple-element.21.refs_3_, ...), custom_call_target="tpu_custom_call" | custom-call | tf_op jit(solution)/shard_map/final_part/pallas_call | solution.py:297
Async XLA Ops:
  0.0 0.9 %copy-start.2 = (f32[512,128]{1,0:T(8,128)S(1)}, f32[512,128]{1,0:T(8,128)}, u32[]{:S(2)}) copy-start(f32[512,128]{1,0:T(8,128)} %moving.1) | copy-start | bytes 786436
  1.0 0.9 %copy-start.3 = (f32[512,128]{1,0:T(8,128)S(1)}, f32[512,128]{1,0:T(8,128)}, u32[]{:S(2)}) copy-start(f32[512,128]{1,0:T(8,128)} %fixed.1) | copy-start | bytes 786436
  1.9 11.9 %copy-start = (s32[2,128,512]{2,1,0:T(8,128)S(1)}, s32[2,128,512]{2,1,0:T(8,128)}, u32[]{:S(2)}) copy-start(s32[2,128,512]{2,1,0:T(8,128)} %refs_4_.1) | copy-start | bytes 1572868
  2.0 8.5 %collective-permute-start.3 = (f32[136,128]{1,0:T(8,128)S(1)}, f32[136,128]{1,0:T(8,128)S(1)}, u32[]{:S(2)}, u32[]{:S(2)}) collective-permute-start(f32[136,128]{1,0:T(8,128)S(1)} %get-tuple-element.22), channel_id=1, source_target_pairs={{0,2},{1,3},{2,0},{3,1},{4,6},{5,7},{6,4},{7,5},{8,10},{9,11},{10,... | collective-permute-start | bytes 208904 | tf_op jit(solution)/shard_map/ppermute | solution.py:268
  6.1 7.7 %collective-permute-start.4 = (f32[136,128]{1,0:T(8,128)S(1)}, f32[136,128]{1,0:T(8,128)S(1)}, u32[]{:S(2)}, u32[]{:S(2)}) collective-permute-start(f32[136,128]{1,0:T(8,128)S(1)} %get-tuple-element.23), channel_id=1, source_target_pairs={{0,1},{1,2},{2,3},{3,0},{4,5},{5,6},{6,7},{7,4},{8,9},{9,10},{10,1... | collective-permute-start | bytes 208904 | tf_op jit(solution)/shard_map/ppermute | solution.py:268
  7.7 6.1 %collective-permute-start.5 = (f32[136,128]{1,0:T(8,128)S(1)}, f32[136,128]{1,0:T(8,128)S(1)}, u32[]{:S(2)}, u32[]{:S(2)}) collective-permute-start(f32[136,128]{1,0:T(8,128)S(1)} %get-tuple-element.24), channel_id=1, source_target_pairs={{0,3},{1,0},{2,1},{3,2},{4,7},{5,4},{6,5},{7,6},{8,11},{9,8},{10,9... | collective-permute-start | bytes 208904 | tf_op jit(solution)/shard_map/ppermute | solution.py:268
  10.0 7.6 %collective-permute-start = (f32[136,128]{1,0:T(8,128)S(1)}, f32[136,128]{1,0:T(8,128)S(1)}, u32[]{:S(2)}, u32[]{:S(2)}) collective-permute-start(f32[136,128]{1,0:T(8,128)S(1)} %get-tuple-element.18), channel_id=1, source_target_pairs={{0,2},{1,3},{2,0},{3,1},{4,6},{5,7},{6,4},{7,5},{8,10},{9,11},{10,... | collective-permute-start | bytes 208904 | tf_op jit(solution)/shard_map/ppermute | solution.py:268
  10.0 7.6 %collective-permute-start.1 = (f32[136,128]{1,0:T(8,128)S(1)}, f32[136,128]{1,0:T(8,128)S(1)}, u32[]{:S(2)}, u32[]{:S(2)}) collective-permute-start(f32[136,128]{1,0:T(8,128)S(1)} %get-tuple-element.19), channel_id=1, source_target_pairs={{0,1},{1,2},{2,3},{3,0},{4,5},{5,6},{6,7},{7,4},{8,9},{9,10},{10,1... | collective-permute-start | bytes 208904 | tf_op jit(solution)/shard_map/ppermute | solution.py:268
  10.5 7.2 %collective-permute-start.2 = (f32[136,128]{1,0:T(8,128)S(1)}, f32[136,128]{1,0:T(8,128)S(1)}, u32[]{:S(2)}, u32[]{:S(2)}) collective-permute-start(f32[136,128]{1,0:T(8,128)S(1)} %get-tuple-element.20), channel_id=1, source_target_pairs={{0,3},{1,0},{2,1},{3,2},{4,7},{5,4},{6,5},{7,6},{8,11},{9,8},{10,9... | collective-permute-start | bytes 208904 | tf_op jit(solution)/shard_map/ppermute | solution.py:268
  13.8 1.0 %copy-start.1 = (f32[2,128,512]{2,1,0:T(8,128)S(1)}, f32[2,128,512]{2,1,0:T(8,128)}, u32[]{:S(2)}) copy-start(f32[2,128,512]{2,1,0:T(8,128)} %refs_5_.1) | copy-start | bytes 1572868

commit v3 on v2

--- a/solution.py
+++ b/solution.py
@@ -22,28 +22,40 @@
     return [middle] + [k for k in range(1, n) if k != middle]
 
 
-def pack_band(strip, out, band, n, rows):
-    top = strip[pl.ds(pl.multiple_of(jnp.maximum(band * rows - SUB, 0), SUB), SUB), :]
+def pack_band(strip, base, out, band, n, rows):
+    start = pl.multiple_of(band * rows - base, SUB)
+    size = strip.shape[0]
+    top = strip[pl.ds(pl.multiple_of(jnp.maximum(start - SUB, 0), SUB), SUB), :]
     out[0:HALO, :] = jnp.where(band > 0, top, 0.0)[SUB - HALO :, :]
-    start = pl.multiple_of(band * rows, SUB)
     out[HALO : HALO + rows, :] = strip[pl.ds(start, rows), :]
-    low = strip[pl.ds(pl.multiple_of(jnp.minimum(start + rows, n * rows - SUB), SUB), SUB), :]
+    low = strip[pl.ds(pl.multiple_of(jnp.minimum(start + rows, size - SUB), SUB), SUB), :]
     out[HALO + rows :, :] = jnp.where(band < n - 1, low, 0.0)[:HALO, :]
 
 
-def pack_kernel(n, rows, moving, fixed, *refs):
-    outs, (mbuf, fbuf, sem) = refs[: 2 * n], refs[2 * n :]
+def first_kernel(n, rows, pieces, moving, out, window, sem):
+    band = lax.rem(lax.axis_index("tile") + hops(n)[0], n)
+    size = window.shape[0]
+    base = pl.multiple_of(jnp.clip(band * rows - SUB, 0, n * rows - size), SUB)
+    per = size // pieces
+    copies = [
+        pltpu.make_async_copy(
+            moving.at[pl.ds(pl.multiple_of(base + i * per, SUB), per), :],
+            window.at[pl.ds(i * per, per), :],
+            sem.at[i],
+        )
+        for i in range(pieces)
+    ]
+    for copy in copies:
+        copy.start()
+    for copy in copies:
+        copy.wait()
+    pack_band(window, base, out, band, n, rows)
+
+
+def pack_kernel(n, rows, shifts, strip, *outs):
     me = lax.axis_index("tile")
-    copies = [
-        pltpu.make_async_copy(moving, mbuf, sem.at[0]),
-        pltpu.make_async_copy(fixed, fbuf, sem.at[1]),
-    ]
-    for copy in copies:
-        copy.start()
-    for image, buf in enumerate((mbuf, fbuf)):
-        copies[image].wait()
-        for place, k in enumerate(hops(n) + [0]):
-            pack_band(buf, outs[image * n + place], lax.rem(me + k, n), n, rows)
+    for out, k in zip(outs, shifts):
+        pack_band(strip, 0, out, lax.rem(me + k, n), n, rows)
 
 
 def row_sums(ref, out, rows):
@@ -246,22 +258,41 @@
     return pltpu.with_memory_space_constraint(x, pltpu.VMEM)
 
 
+def far(x):
+    return pltpu.with_memory_space_constraint(x, pltpu.HBM)
+
+
 def on_device(n, fixed, moving, offsets, fractions):
     rows, width = offsets.shape[1:]
     strip = moving.shape
     deep = rows + 2 * HALO
     band = held((deep, strip[1]))
     plane = held((rows, width))
-    packed = pl.pallas_call(
-        functools.partial(pack_kernel, n, rows),
-        out_shape=[band] * (2 * n),
-        in_specs=[ANY] * 2,
-        out_specs=[VMEM] * (2 * n),
-        scratch_shapes=[pltpu.VMEM(strip, F32)] * 2 + [pltpu.SemaphoreType.DMA((2,))],
-        compiler_params=pltpu.CompilerParams(vmem_limit_bytes=ROOM),
-        name="pack",
-    )(moving, fixed)
+    params = pltpu.CompilerParams(vmem_limit_bytes=ROOM)
+    pieces = 3
+    first = pl.pallas_call(
+        functools.partial(first_kernel, n, rows, pieces),
+        out_shape=band,
+        in_specs=[ANY],
+        out_specs=VMEM,
+        scratch_shapes=[
+            pltpu.VMEM((rows + 2 * SUB, strip[1]), F32),
+            pltpu.SemaphoreType.DMA((pieces,)),
+        ],
+        compiler_params=params,
+        name="first",
+    )(far(moving))
     order = hops(n)
+
+    def pack(image, shifts):
+        return pl.pallas_call(
+            functools.partial(pack_kernel, n, rows, shifts),
+            out_shape=[band] * len(shifts),
+            in_specs=[VMEM],
+            out_specs=[VMEM] * len(shifts),
+            compiler_params=params,
+            name="pack",
+        )(near(image))
 
     def send(blocks):
         got = [
@@ -270,8 +301,8 @@
         ]
         return got + [blocks[-1]]
 
-    moved = send(packed[:n])
-    fixes = send(packed[n:])
+    moved = send([first, *pack(moving, order[1:] + [0])])
+    fixes = send(pack(fixed, order + [0]))
     parts = pl.pallas_call(
         functools.partial(moving_kernel, n, rows, width),
         out_shape=[plane] * 5,
@@ -293,7 +324,7 @@
             flops=200 * rows * width, bytes_accessed=16 * rows * width, transcendentals=0
         ),
         name="moving_part",
-    )(*map(near, moved), offsets, fractions)
+    )(*map(near, moved), far(offsets), far(fractions))
     return pl.pallas_call(
         functools.partial(final_kernel, n, rows, width),
         out_shape=jax.ShapeDtypeStruct((rows, width), F32),

time: 19.8 us -> 18.8 us (0.949)
  local copies, waits for them, and re-layouts: 2.94 us -> 0.01 us
  Pallas kernels: 4 us -> 5.88 us
  starting transfers between devices: 11.8 us -> 12 us
    unnamed x8 -> x4, local copies, waits for them, and re-layouts: 2.94 us -> 0.01 us
    pallas_call x1, Pallas kernels: 1.97 us -> 3.03 us  [on_device(): pl.pallas_call(functools.partial(moving_kernel, n, rows, width), out_shap...]
    pallas_call x1 -> x3, Pallas kernels: 0.1 us -> 0.9 us  [the longest x1 0.86 us: on_device(): pl.pallas_call(functools.partial(first_kernel, n, rows, pieces), out_shap...]
  transfers between devices with their start and end apart: 6 -> 6, of which waited for: 2 -> 2; matrix products, arithmetic and copies ran while one was open for 0% -> 0% of each run, Pallas kernels for 10% -> 17%
where the time goes in v3:
time: 18.8 us; the launch traced here: 18.6 us
  starting transfers between devices  12 us (64%)
  Pallas kernels  5.88 us (31%)
  waiting for transfers between devices  0.76 us (4%)
    ppermute x6, starting transfers between devices, send(): lax.ppermute(block, 'tile', [(i, (i + k) % n) for i in range(n)])  12 us
    pallas_call x1, Pallas kernels, on_device(): pl.pallas_call(functools.partial(moving_kernel, n, rows, width), out_shap...  3.03 us
    pallas_call x1, Pallas kernels, on_device(): pl.pallas_call(functools.partial(final_kernel, n, rows, width), out_shape...  1.95 us
    pallas_call x1, Pallas kernels, on_device(): pl.pallas_call(functools.partial(first_kernel, n, rows, pieces), out_shap...  0.86 us
    ppermute x6, waiting for transfers between devices, send(): lax.ppermute(block, 'tile', [(i, (i + k) % n) for i in range(n)])  0.76 us
  transfers between devices with their start and end apart: 6, of which 2 were waited for; matrix products, arithmetic and copies ran while one was open for 0% of the time, Pallas kernels for 17%

profile of v3, /device:TPU:0, one launch (start us, length us, event | category | flops | bytes accessed | tf_op | source)
XLA Modules:
  0.0 18.6 jit_solution(14954646481087091866)
XLA Ops:
  0.0 0.0 copy-start
  0.0 0.0 copy-start.1
  0.0 0.9 %first.1 = f32[136,128]{1,0:T(8,128)S(1)} custom-call(f32[512,128]{1,0:T(8,128)} %strip.3), custom_call_target="tpu_custom_call" | custom-call | tf_op jit(solution)/shard_map/first/pallas_call | solution.py:273
  0.9 4.1 %collective-permute-start.3 = (f32[136,128]{1,0:T(8,128)S(1)}, f32[136,128]{1,0:T(8,128)S(1)}, u32[]{:S(2)}, u32[]{:S(2)}) collective-permute-start(f32[136,128]{1,0:T(8,128)S(1)} %first.1), channel_id=1, source_target_pairs={{0,2},{1,3},{2,0},{3,1},{4,6},{5,7},{6,4},{7,5},{8,10},{9,11},{10,... | collective-permute-start | bytes 208904 | tf_op jit(solution)/shard_map/ppermute | solution.py:299
  5.0 0.0 copy-done
  5.0 1.6 %collective-permute-start.4 = (f32[136,128]{1,0:T(8,128)S(1)}, f32[136,128]{1,0:T(8,128)S(1)}, u32[]{:S(2)}, u32[]{:S(2)}) collective-permute-start(f32[136,128]{1,0:T(8,128)S(1)} %get-tuple-element.21), channel_id=1, source_target_pairs={{0,1},{1,2},{2,3},{3,0},{4,5},{5,6},{6,7},{7,4},{8,9},{9,10},{10,1... | collective-permute-start | bytes 208904 | tf_op jit(solution)/shard_map/ppermute | solution.py:299
  6.7 2.2 %collective-permute-start.5 = (f32[136,128]{1,0:T(8,128)S(1)}, f32[136,128]{1,0:T(8,128)S(1)}, u32[]{:S(2)}, u32[]{:S(2)}) collective-permute-start(f32[136,128]{1,0:T(8,128)S(1)} %get-tuple-element.22), channel_id=1, source_target_pairs={{0,3},{1,0},{2,1},{3,2},{4,7},{5,4},{6,5},{7,6},{8,11},{9,8},{10,9... | collective-permute-start | bytes 208904 | tf_op jit(solution)/shard_map/ppermute | solution.py:299
  8.9 0.0 copy-done.1
  8.9 0.1 collective-permute-start
  9.0 0.6 %collective-permute-start.1 = (f32[136,128]{1,0:T(8,128)S(1)}, f32[136,128]{1,0:T(8,128)S(1)}, u32[]{:S(2)}, u32[]{:S(2)}) collective-permute-start(f32[136,128]{1,0:T(8,128)S(1)} %get-tuple-element.18), channel_id=1, source_target_pairs={{0,1},{1,2},{2,3},{3,0},{4,5},{5,6},{6,7},{7,4},{8,9},{9,10},{10,1... | collective-permute-start | bytes 208904 | tf_op jit(solution)/shard_map/ppermute | solution.py:299
  9.6 0.0 collective-permute-done.3.refs_0_.refs_4_
  9.6 3.3 %collective-permute-start.2 = (f32[136,128]{1,0:T(8,128)S(1)}, f32[136,128]{1,0:T(8,128)S(1)}, u32[]{:S(2)}, u32[]{:S(2)}) collective-permute-start(f32[136,128]{1,0:T(8,128)S(1)} %get-tuple-element.19), channel_id=1, source_target_pairs={{0,3},{1,0},{2,1},{3,2},{4,7},{5,4},{6,5},{7,6},{8,11},{9,8},{10,9... | collective-permute-start | bytes 208904 | tf_op jit(solution)/shard_map/ppermute | solution.py:299
  12.9 0.0 collective-permute-done.4.refs_1_.refs_5_
  12.9 0.0 collective-permute-done.5.refs_2_.refs_6_
  12.9 3.0 %moving_part.1 = (f32[128,512]{1,0:T(8,128)S(1)}, f32[128,512]{1,0:T(8,128)S(1)}, f32[128,512]{1,0:T(8,128)S(1)}, f32[128,512]{1,0:T(8,128)S(1)}, f32[128,512]{1,0:T(8,128)S(1)}) custom-call(f32[136,128]{1,0:T(8,128)S(1)} %collective-permute-done.3.refs_0_.refs_4_, f32[136,128]{1,0:T(8,128)S(1)} %collective-permute-done.4.refs_1_.refs_5_, ...), custom_call_target="tpu_custom_call" | custom-call | flops 13107200 | bytes 1048576 | tf_op jit(solution)/shard_map/moving_part/pallas_call | solution.py:306
  15.9 0.6 %collective-permute-done.refs_0_ = f32[136,128]{1,0:T(8,128)S(1)} collective-permute-done((f32[136,128]{1,0:T(8,128)S(1)}, f32[136,128]{1,0:T(8,128)S(1)}, u32[]{:S(2)}, u32[]{:S(2)}) %collective-permute-start) | collective-permute-done | bytes 69664 | tf_op jit(solution)/shard_map/ppermute | solution.py:299
  16.5 0.0 collective-permute-done.1.refs_1_
  16.5 0.2 collective-permute-done.2.refs_2_
  16.7 2.0 %final_part.1 = f32[128,512]{1,0:T(8,128)} custom-call(f32[136,128]{1,0:T(8,128)S(1)} %collective-permute-done.refs_0_, f32[136,128]{1,0:T(8,128)S(1)} %collective-permute-done.1.refs_1_, f32[136,128]{1,0:T(8,128)S(1)} %collective-permute-done.2.refs_2_, f32[136,128]{1,0:T(8,128)S(1)} %get-tuple-element.20.refs_3_, ...), custom_call_target="tpu_custom_call" | custom-call | tf_op jit(solution)/shard_map/final_part/pallas_call | solution.py:328
  (2 shorter events, 0.0 us)
Async XLA Ops:
  0.0 5.0 %copy-start = (f32[512,128]{1,0:T(8,128)S(1)}, f32[512,128]{1,0:T(8,128)}, u32[]{:S(2)}) copy-start(f32[512,128]{1,0:T(8,128)} %strip.3) | copy-start | bytes 786436
  0.0 8.9 %copy-start.1 = (f32[512,128]{1,0:T(8,128)S(1)}, f32[512,128]{1,0:T(8,128)}, u32[]{:S(2)}) copy-start(f32[512,128]{1,0:T(8,128)} %strip.2) | copy-start | bytes 786436
  0.9 8.7 %collective-permute-start.3 = (f32[136,128]{1,0:T(8,128)S(1)}, f32[136,128]{1,0:T(8,128)S(1)}, u32[]{:S(2)}, u32[]{:S(2)}) collective-permute-start(f32[136,128]{1,0:T(8,128)S(1)} %first.1), channel_id=1, source_target_pairs={{0,2},{1,3},{2,0},{3,1},{4,6},{5,7},{6,4},{7,5},{8,10},{9,11},{10,... | collective-permute-start | bytes 208904 | tf_op jit(solution)/shard_map/ppermute | solution.py:299
  5.0 7.9 %collective-permute-start.4 = (f32[136,128]{1,0:T(8,128)S(1)}, f32[136,128]{1,0:T(8,128)S(1)}, u32[]{:S(2)}, u32[]{:S(2)}) collective-permute-start(f32[136,128]{1,0:T(8,128)S(1)} %get-tuple-element.21), channel_id=1, source_target_pairs={{0,1},{1,2},{2,3},{3,0},{4,5},{5,6},{6,7},{7,4},{8,9},{9,10},{10,1... | collective-permute-start | bytes 208904 | tf_op jit(solution)/shard_map/ppermute | solution.py:299
  6.7 6.2 %collective-permute-start.5 = (f32[136,128]{1,0:T(8,128)S(1)}, f32[136,128]{1,0:T(8,128)S(1)}, u32[]{:S(2)}, u32[]{:S(2)}) collective-permute-start(f32[136,128]{1,0:T(8,128)S(1)} %get-tuple-element.22), channel_id=1, source_target_pairs={{0,3},{1,0},{2,1},{3,2},{4,7},{5,4},{6,5},{7,6},{8,11},{9,8},{10,9... | collective-permute-start | bytes 208904 | tf_op jit(solution)/shard_map/ppermute | solution.py:299
  8.9 7.6 %collective-permute-start = (f32[136,128]{1,0:T(8,128)S(1)}, f32[136,128]{1,0:T(8,128)S(1)}, u32[]{:S(2)}, u32[]{:S(2)}) collective-permute-start(f32[136,128]{1,0:T(8,128)S(1)} %get-tuple-element.17), channel_id=1, source_target_pairs={{0,2},{1,3},{2,0},{3,1},{4,6},{5,7},{6,4},{7,5},{8,10},{9,11},{10,... | collective-permute-start | bytes 208904 | tf_op jit(solution)/shard_map/ppermute | solution.py:299
  9.0 7.5 %collective-permute-start.1 = (f32[136,128]{1,0:T(8,128)S(1)}, f32[136,128]{1,0:T(8,128)S(1)}, u32[]{:S(2)}, u32[]{:S(2)}) collective-permute-start(f32[136,128]{1,0:T(8,128)S(1)} %get-tuple-element.18), channel_id=1, source_target_pairs={{0,1},{1,2},{2,3},{3,0},{4,5},{5,6},{6,7},{7,4},{8,9},{9,10},{10,1... | collective-permute-start | bytes 208904 | tf_op jit(solution)/shard_map/ppermute | solution.py:299
  9.6 7.1 %collective-permute-start.2 = (f32[136,128]{1,0:T(8,128)S(1)}, f32[136,128]{1,0:T(8,128)S(1)}, u32[]{:S(2)}, u32[]{:S(2)}) collective-permute-start(f32[136,128]{1,0:T(8,128)S(1)} %get-tuple-element.19), channel_id=1, source_target_pairs={{0,3},{1,0},{2,1},{3,2},{4,7},{5,4},{6,5},{7,6},{8,11},{9,8},{10,9... | collective-permute-start | bytes 208904 | tf_op jit(solution)/shard_map/ppermute | solution.py:299

commit v4 on v3

--- a/solution.py
+++ b/solution.py
@@ -120,10 +120,59 @@
     return [jnp.where(bit, values[i + 4], values[i]) for i in range(4)] + [values[4]]
 
 
+def fixed_row_sums(f, m, products, rows):
+    for y in range(0, f.shape[0], SUB):
+        x = f[y : y + SUB, :]
+        products[0, y : y + SUB, :] = x * x
+        products[1, y : y + SUB, :] = x * m[y : y + SUB, :]
+    return [
+        row_sums(ref, products.at[2 + which], rows)
+        for which, ref in enumerate((f, products.at[0], products.at[1]))
+    ]
+
+
+def lane_windows(terms, out):
+    arrays, _, rows, width = terms.shape
+    blocks = width // LANES
+    size = LANES * (2 if blocks % 2 == 0 else 1)
+    source = lax.broadcasted_iota(jnp.int32, (size, size), 0)
+    target = lax.broadcasted_iota(jnp.int32, (size, size), 1)
+    near_by = (source - target <= RADIUS) & (target - source <= RADIUS)
+    inside = jnp.where(near_by, 1.0, 0.0).astype(BF16)
+    source = lax.broadcasted_iota(jnp.int32, (2 * LANES, 2 * LANES), 0)
+    target = lax.broadcasted_iota(jnp.int32, (2 * LANES, 2 * LANES), 1)
+    near_by = (source - target <= RADIUS) & (target - source <= RADIUS)
+    other = (source < LANES) != (target < LANES)
+    across = jnp.where(near_by & other, 1.0, 0.0).astype(BF16)
+
+    def times(starts, wide, weights):
+        left = [
+            jnp.concatenate([terms[a, t, :, start : start + wide] for t in range(3)], axis=1)
+            for a in range(arrays)
+            for start in starts
+        ]
+        got = jnp.dot(
+            jnp.concatenate(left, axis=0),
+            jnp.concatenate([weights] * 3, axis=0),
+            preferred_element_type=F32,
+        )
+        for i in range(len(left)):
+            yield divmod(i, len(starts)), got[i * rows : (i + 1) * rows]
+
+    starts = list(range(0, width, size))
+    for (a, place), part in times(starts, size, inside):
+        out[a, :, starts[place] : starts[place] + size] = part
+    starts = [start - LANES for start in starts[1:]]
+    if starts:
+        for (a, place), part in times(starts, 2 * LANES, across):
+            at = slice(starts[place], starts[place] + 2 * LANES)
+            out[a, :, at] = out[a, :, at] + part
+
+
 def moving_kernel(n, rows, width, *refs):
-    blocks, offsets, fractions = refs[:n], refs[n], refs[n + 1]
-    base, linear, square, msum, mvar = refs[n + 2 : n + 7]
-    image, sums, squares, shifted, sq, three, obuf, fbuf, sem = refs[n + 7 :]
+    blocks, fixed, offsets, fractions = refs[:n], refs[n], refs[n + 1], refs[n + 2]
+    base, linear, square, msum, mvar, own = refs[n + 3 : n + 9]
+    image, sums, squares, shifted, sq, three, products, obuf, fbuf, sem = refs[n + 9 :]
     me = lax.axis_index("tile")
     copies = [
         pltpu.make_async_copy(offsets, obuf, sem.at[0]),
@@ -131,6 +180,8 @@
     ]
     for copy in copies:
         copy.start()
+    for which, total in enumerate(fixed_row_sums(fixed, blocks[n - 1], products, rows)):
+        own[which] = total(0, rows)
     deep = rows + 2 * HALO
     inv = 1.0 / float((2 * RADIUS + 1) ** 2)
     for terms in (sums, squares):
@@ -208,38 +259,46 @@
             unit(s, g * SUB)
 
 
-def final_kernel(n, rows, width, *refs):
-    fixed, moving = refs[:n], refs[n : 2 * n]
-    base, linear, square, msum, mvar, out = refs[2 * n : 2 * n + 6]
-    sums, squares, crosses, ff, fm, three, obuf, sem = refs[2 * n + 6 :]
+def final_kernel(n, rows, width, chunks, *refs):
+    fixed, moving = refs[: n - 1], refs[n - 1 : 2 * n - 2]
+    base, linear, square, msum, mvar, own, out = refs[2 * n - 2 : 2 * n + 5]
+    summed, triple, terms, windows, products, obuf, sem = refs[2 * n + 5 :]
     me = lax.axis_index("tile")
     inv = 1.0 / float((2 * RADIUS + 1) ** 2)
-    for terms in (sums, squares, crosses):
-        clear_ends(terms)
-    for place, k in enumerate(hops(n) + [0]):
-        f, m = fixed[place], moving[place]
-        source = lax.rem(me - k + n, n)
-        for y in range(0, rows + 2 * HALO, SUB):
-            x = f[y : y + SUB, :]
-            ff[place, y : y + SUB, :] = x * x
-            fm[place, y : y + SUB, :] = x * m[y : y + SUB, :]
-        for which, (ref, terms) in enumerate(
-            ((f, sums), (ff.at[place], squares), (fm.at[place], crosses))
-        ):
-            total = row_sums(ref, three.at[which, place], rows)
-            for y in range(0, rows, 2 * SUB):
-                put(terms, source, y, total(y, 2 * SUB))
-    size = LANES * (2 if n % 2 == 0 else 1)
-    window = band_matrix(-RADIUS, RADIUS, size)
+    extent = width + LANES
+    summed[:, width:] = jnp.zeros((rows, LANES), F32)
+
+    def keep(source, totals):
+        at = pl.ds(pl.multiple_of(source * LANES, LANES), LANES)
+        for y in range(0, rows, 2 * SUB):
+            summed[y : y + 2 * SUB, at] = totals[0](y, 2 * SUB)
+            for which in range(2):
+                for t, part in enumerate(split(totals[1 + which](y, 2 * SUB))):
+                    terms[which, t, y : y + 2 * SUB, at] = part
+
+    keep(me, [lambda y, size, w=w: own[w, y : y + size, :] for w in range(3)])
+    for place, k in enumerate(hops(n)):
+        keep(
+            lax.rem(me - k + n, n),
+            fixed_row_sums(fixed[place], moving[place], products.at[place], rows),
+        )
+    lane_windows(terms, windows)
+    for y in range(0, rows, SUB):
+        x = summed[y : y + SUB, :]
+        triple[y : y + SUB, :] = x + pltpu.roll(x, 1, 1) + pltpu.roll(x, extent - 1, 1)
+    per = rows // chunks
     copies = []
-    windows = lane_sums((sums, squares, crosses), width, size, window)
-    for place, (fsum, second, cross) in enumerate(zip(*windows)):
-        at = pl.ds(place * size, size)
-        fvar = second - fsum * fsum * inv
-        cov = cross - fsum * msum[:, at] * inv
-        conf = 0.5 + 0.5 * (cov * lax.rsqrt(fvar * mvar[:, at] + 0.001))
-        obuf[:, at] = base[:, at] + conf * (linear[:, at] + conf * square[:, at])
-        copy = pltpu.make_async_copy(obuf.at[:, at], out.at[:, at], sem.at[place])
+    for chunk in range(chunks):
+        for y in range(chunk * per, (chunk + 1) * per, SUB):
+            at = slice(y, y + SUB)
+            x = triple[at, :]
+            fsum = (x + pltpu.roll(x, 3, 1) + pltpu.roll(x, extent - 3, 1))[:, :width]
+            fvar = windows[0, at, :] - fsum * fsum * inv
+            cov = windows[1, at, :] - fsum * msum[at, :] * inv
+            conf = 0.5 + 0.5 * (cov * lax.rsqrt(fvar * mvar[at, :] + 0.001))
+            obuf[at, :] = base[at, :] + conf * (linear[at, :] + conf * square[at, :])
+        span = pl.ds(chunk * per, per)
+        copy = pltpu.make_async_copy(obuf.at[span, :], out.at[span, :], sem.at[chunk])
         copy.start()
         copies.append(copy)
     for copy in copies:
@@ -305,9 +364,9 @@
     fixes = send(pack(fixed, order + [0]))
     parts = pl.pallas_call(
         functools.partial(moving_kernel, n, rows, width),
-        out_shape=[plane] * 5,
-        in_specs=[VMEM] * n + [ANY] * 2,
-        out_specs=[VMEM] * 5,
+        out_shape=[plane] * 5 + [held((3, rows, strip[1]))],
+        in_specs=[VMEM] * (n + 1) + [ANY] * 2,
+        out_specs=[VMEM] * 6,
         scratch_shapes=[
             pltpu.VMEM((deep, width + LANES), F32),
             pltpu.VMEM((3, rows, width + 2 * LANES), BF16),
@@ -315,34 +374,35 @@
             pltpu.VMEM((n, 2 * REACH + 2, deep, LANES), F32),
             pltpu.VMEM((n, deep, LANES), F32),
             pltpu.VMEM((2, n, deep, LANES), F32),
+            pltpu.VMEM((5, deep, LANES), F32),
             pltpu.VMEM(offsets.shape, jnp.int32),
             pltpu.VMEM(fractions.shape, F32),
             pltpu.SemaphoreType.DMA((2,)),
         ],
-        compiler_params=pltpu.CompilerParams(vmem_limit_bytes=ROOM),
+        compiler_params=params,
         cost_estimate=pl.CostEstimate(
             flops=200 * rows * width, bytes_accessed=16 * rows * width, transcendentals=0
         ),
         name="moving_part",
-    )(*map(near, moved), far(offsets), far(fractions))
+    )(*map(near, (*moved, fixes[-1])), far(offsets), far(fractions))
+    chunks = 4
     return pl.pallas_call(
-        functools.partial(final_kernel, n, rows, width),
+        functools.partial(final_kernel, n, rows, width, chunks),
         out_shape=jax.ShapeDtypeStruct((rows, width), F32),
-        in_specs=[VMEM] * (2 * n + 5),
+        in_specs=[VMEM] * (2 * n + 4),
         out_specs=ANY,
         scratch_shapes=[
-            pltpu.VMEM((3, rows, width + 2 * LANES), BF16),
-            pltpu.VMEM((3, rows, width + 2 * LANES), BF16),
-            pltpu.VMEM((3, rows, width + 2 * LANES), BF16),
-            pltpu.VMEM((n, deep, LANES), F32),
-            pltpu.VMEM((n, deep, LANES), F32),
-            pltpu.VMEM((3, n, deep, LANES), F32),
+            pltpu.VMEM((rows, width + LANES), F32),
+            pltpu.VMEM((rows, width + LANES), F32),
+            pltpu.VMEM((2, 3, rows, width), BF16),
+            pltpu.VMEM((2, rows, width), F32),
+            pltpu.VMEM((n - 1, 5, deep, LANES), F32),
             pltpu.VMEM((rows, width), F32),
-            pltpu.SemaphoreType.DMA((n,)),
+            pltpu.SemaphoreType.DMA((chunks,)),
         ],
-        compiler_params=pltpu.CompilerParams(vmem_limit_bytes=ROOM),
+        compiler_params=params,
         name="final_part",
-    )(*map(near, (*fixes, *moved, *parts)))
+    )(*map(near, (*fixes[:-1], *moved[:-1], *parts)))
 
 
 def solution(mesh):

time: 18.8 us -> 18.5 us (0.984)
  Pallas kernels: 5.88 us -> 5.61 us
    pallas_call x1, Pallas kernels: 1.95 us -> 1.7 us  [on_device(): pl.pallas_call(functools.partial(final_kernel, n, rows, width, chunks), o...]
where the time goes in v4:
time: 18.5 us; the launch traced here: 18.4 us
  starting transfers between devices  12 us (65%)
  Pallas kernels  5.61 us (30%)
  waiting for transfers between devices  0.78 us (4%)
    ppermute x6, starting transfers between devices, send(): lax.ppermute(block, 'tile', [(i, (i + k) % n) for i in range(n)])  12 us
    pallas_call x1, Pallas kernels, on_device(): pl.pallas_call(functools.partial(moving_kernel, n, rows, width), out_shap...  3.01 us
    pallas_call x1, Pallas kernels, on_device(): pl.pallas_call(functools.partial(final_kernel, n, rows, width, chunks), o...  1.7 us
    pallas_call x1, Pallas kernels, on_device(): pl.pallas_call(functools.partial(first_kernel, n, rows, pieces), out_shap...  0.86 us
    ppermute x6, waiting for transfers between devices, send(): lax.ppermute(block, 'tile', [(i, (i + k) % n) for i in range(n)])  0.78 us
  transfers between devices with their start and end apart: 6, of which 2 were waited for; matrix products, arithmetic and copies ran while one was open for 0% of the time, Pallas kernels for 17%

profile of v4, /device:TPU:0, one launch (start us, length us, event | category | flops | bytes accessed | tf_op | source)
XLA Modules:
  0.0 18.4 jit_solution(7397775640346412721)
XLA Ops:
  0.0 0.0 copy-start
  0.0 0.0 copy-start.1
  0.0 0.9 %first.1 = f32[136,128]{1,0:T(8,128)S(1)} custom-call(f32[512,128]{1,0:T(8,128)} %strip.3), custom_call_target="tpu_custom_call" | custom-call | tf_op jit(solution)/shard_map/first/pallas_call | solution.py:332
  0.9 4.1 %collective-permute-start.3 = (f32[136,128]{1,0:T(8,128)S(1)}, f32[136,128]{1,0:T(8,128)S(1)}, u32[]{:S(2)}, u32[]{:S(2)}) collective-permute-start(f32[136,128]{1,0:T(8,128)S(1)} %first.1), channel_id=1, source_target_pairs={{0,2},{1,3},{2,0},{3,1},{4,6},{5,7},{6,4},{7,5},{8,10},{9,11},{10,... | collective-permute-start | bytes 208904 | tf_op jit(solution)/shard_map/ppermute | solution.py:358
  5.0 0.0 copy-done
  5.0 1.6 %collective-permute-start.4 = (f32[136,128]{1,0:T(8,128)S(1)}, f32[136,128]{1,0:T(8,128)S(1)}, u32[]{:S(2)}, u32[]{:S(2)}) collective-permute-start(f32[136,128]{1,0:T(8,128)S(1)} %get-tuple-element.21), channel_id=1, source_target_pairs={{0,1},{1,2},{2,3},{3,0},{4,5},{5,6},{6,7},{7,4},{8,9},{9,10},{10,1... | collective-permute-start | bytes 208904 | tf_op jit(solution)/shard_map/ppermute | solution.py:358
  6.7 2.2 %collective-permute-start.5 = (f32[136,128]{1,0:T(8,128)S(1)}, f32[136,128]{1,0:T(8,128)S(1)}, u32[]{:S(2)}, u32[]{:S(2)}) collective-permute-start(f32[136,128]{1,0:T(8,128)S(1)} %get-tuple-element.22), channel_id=1, source_target_pairs={{0,3},{1,0},{2,1},{3,2},{4,7},{5,4},{6,5},{7,6},{8,11},{9,8},{10,9... | collective-permute-start | bytes 208904 | tf_op jit(solution)/shard_map/ppermute | solution.py:358
  8.9 0.0 copy-done.1
  8.9 0.1 collective-permute-start
  9.0 0.6 %collective-permute-start.1 = (f32[136,128]{1,0:T(8,128)S(1)}, f32[136,128]{1,0:T(8,128)S(1)}, u32[]{:S(2)}, u32[]{:S(2)}) collective-permute-start(f32[136,128]{1,0:T(8,128)S(1)} %get-tuple-element.19), channel_id=1, source_target_pairs={{0,1},{1,2},{2,3},{3,0},{4,5},{5,6},{6,7},{7,4},{8,9},{9,10},{10,1... | collective-permute-start | bytes 208904 | tf_op jit(solution)/shard_map/ppermute | solution.py:358
  9.6 0.0 collective-permute-done.3.refs_0_.refs_3_
  9.6 3.3 %collective-permute-start.2 = (f32[136,128]{1,0:T(8,128)S(1)}, f32[136,128]{1,0:T(8,128)S(1)}, u32[]{:S(2)}, u32[]{:S(2)}) collective-permute-start(f32[136,128]{1,0:T(8,128)S(1)} %get-tuple-element.20), channel_id=1, source_target_pairs={{0,3},{1,0},{2,1},{3,2},{4,7},{5,4},{6,5},{7,6},{8,11},{9,8},{10,9... | collective-permute-start | bytes 208904 | tf_op jit(solution)/shard_map/ppermute | solution.py:358
  12.9 0.0 collective-permute-done.4.refs_1_.refs_4_
  12.9 0.0 collective-permute-done.5.refs_2_.refs_5_
  12.9 3.0 %moving_part.1 = (f32[128,512]{1,0:T(8,128)S(1)}, f32[128,512]{1,0:T(8,128)S(1)}, f32[128,512]{1,0:T(8,128)S(1)}, f32[128,512]{1,0:T(8,128)S(1)}, f32[128,512]{1,0:T(8,128)S(1)}, /*index=5*/f32[3,128,128]{2,1,0:T(8,128)S(1)}) custom-call(f32[136,128]{1,0:T(8,128)S(1)} %collective-permute-done.3.refs_0_.refs_3_, ...), custom_call_target="tpu_custom_call" | custom-call | flops 13107200 | bytes 1048576 | tf_op jit(solution)/shard_map/moving_part/pallas_call | solution.py:365
  15.9 0.6 %collective-permute-done.refs_0_ = f32[136,128]{1,0:T(8,128)S(1)} collective-permute-done((f32[136,128]{1,0:T(8,128)S(1)}, f32[136,128]{1,0:T(8,128)S(1)}, u32[]{:S(2)}, u32[]{:S(2)}) %collective-permute-start) | collective-permute-done | bytes 69664 | tf_op jit(solution)/shard_map/ppermute | solution.py:358
  16.5 0.0 collective-permute-done.1.refs_1_
  16.5 0.2 collective-permute-done.2.refs_2_
  16.7 1.7 %final_part.1 = f32[128,512]{1,0:T(8,128)} custom-call(f32[136,128]{1,0:T(8,128)S(1)} %collective-permute-done.refs_0_, f32[136,128]{1,0:T(8,128)S(1)} %collective-permute-done.1.refs_1_, f32[136,128]{1,0:T(8,128)S(1)} %collective-permute-done.2.refs_2_, f32[136,128]{1,0:T(8,128)S(1)} %collective-permute-done.3.refs_0_.refs_3_, ...), custom_call_target="tpu_custom_call" | custom-call | tf_op jit(solution)/shard_map/final_part/pallas_call | solution.py:389
  (2 shorter events, 0.0 us)
Async XLA Ops:
  0.0 5.0 %copy-start = (f32[512,128]{1,0:T(8,128)S(1)}, f32[512,128]{1,0:T(8,128)}, u32[]{:S(2)}) copy-start(f32[512,128]{1,0:T(8,128)} %strip.3) | copy-start | bytes 786436
  0.0 8.9 %copy-start.1 = (f32[512,128]{1,0:T(8,128)S(1)}, f32[512,128]{1,0:T(8,128)}, u32[]{:S(2)}) copy-start(f32[512,128]{1,0:T(8,128)} %strip.2) | copy-start | bytes 786436
  0.9 8.7 %collective-permute-start.3 = (f32[136,128]{1,0:T(8,128)S(1)}, f32[136,128]{1,0:T(8,128)S(1)}, u32[]{:S(2)}, u32[]{:S(2)}) collective-permute-start(f32[136,128]{1,0:T(8,128)S(1)} %first.1), channel_id=1, source_target_pairs={{0,2},{1,3},{2,0},{3,1},{4,6},{5,7},{6,4},{7,5},{8,10},{9,11},{10,... | collective-permute-start | bytes 208904 | tf_op jit(solution)/shard_map/ppermute | solution.py:358
  5.0 7.9 %collective-permute-start.4 = (f32[136,128]{1,0:T(8,128)S(1)}, f32[136,128]{1,0:T(8,128)S(1)}, u32[]{:S(2)}, u32[]{:S(2)}) collective-permute-start(f32[136,128]{1,0:T(8,128)S(1)} %get-tuple-element.21), channel_id=1, source_target_pairs={{0,1},{1,2},{2,3},{3,0},{4,5},{5,6},{6,7},{7,4},{8,9},{9,10},{10,1... | collective-permute-start | bytes 208904 | tf_op jit(solution)/shard_map/ppermute | solution.py:358
  6.7 6.2 %collective-permute-start.5 = (f32[136,128]{1,0:T(8,128)S(1)}, f32[136,128]{1,0:T(8,128)S(1)}, u32[]{:S(2)}, u32[]{:S(2)}) collective-permute-start(f32[136,128]{1,0:T(8,128)S(1)} %get-tuple-element.22), channel_id=1, source_target_pairs={{0,3},{1,0},{2,1},{3,2},{4,7},{5,4},{6,5},{7,6},{8,11},{9,8},{10,9... | collective-permute-start | bytes 208904 | tf_op jit(solution)/shard_map/ppermute | solution.py:358
  8.9 7.6 %collective-permute-start = (f32[136,128]{1,0:T(8,128)S(1)}, f32[136,128]{1,0:T(8,128)S(1)}, u32[]{:S(2)}, u32[]{:S(2)}) collective-permute-start(f32[136,128]{1,0:T(8,128)S(1)} %get-tuple-element.18), channel_id=1, source_target_pairs={{0,2},{1,3},{2,0},{3,1},{4,6},{5,7},{6,4},{7,5},{8,10},{9,11},{10,... | collective-permute-start | bytes 208904 | tf_op jit(solution)/shard_map/ppermute | solution.py:358
  9.0 7.5 %collective-permute-start.1 = (f32[136,128]{1,0:T(8,128)S(1)}, f32[136,128]{1,0:T(8,128)S(1)}, u32[]{:S(2)}, u32[]{:S(2)}) collective-permute-start(f32[136,128]{1,0:T(8,128)S(1)} %get-tuple-element.19), channel_id=1, source_target_pairs={{0,1},{1,2},{2,3},{3,0},{4,5},{5,6},{6,7},{7,4},{8,9},{9,10},{10,1... | collective-permute-start | bytes 208904 | tf_op jit(solution)/shard_map/ppermute | solution.py:358
  9.6 7.1 %collective-permute-start.2 = (f32[136,128]{1,0:T(8,128)S(1)}, f32[136,128]{1,0:T(8,128)S(1)}, u32[]{:S(2)}, u32[]{:S(2)}) collective-permute-start(f32[136,128]{1,0:T(8,128)S(1)} %get-tuple-element.20), channel_id=1, source_target_pairs={{0,3},{1,0},{2,1},{3,2},{4,7},{5,4},{6,5},{7,6},{8,11},{9,8},{10,9... | collective-permute-start | bytes 208904 | tf_op jit(solution)/shard_map/ppermute | solution.py:358

commit v5 on v4

--- a/solution.py
+++ b/solution.py
@@ -17,9 +17,14 @@
 ROOM = 28 * 2**20
 
 
-def hops(n):
-    middle = n // 2
-    return [middle] + [k for k in range(1, n) if k != middle]
+PIECES = 3
+STEPS = 2
+MOVING_ORDER = (2, 1, 3)
+FIXED_ORDER = (2, 1, 3)
+
+
+def hops(n, first=(2, 1, 3)):
+    return list(first) if n == 4 else list(range(1, n))
 
 
 def pack_band(strip, base, out, band, n, rows):
@@ -33,7 +38,7 @@
 
 
 def first_kernel(n, rows, pieces, moving, out, window, sem):
-    band = lax.rem(lax.axis_index("tile") + hops(n)[0], n)
+    band = lax.rem(lax.axis_index("tile") + hops(n, MOVING_ORDER)[0], n)
     size = window.shape[0]
     base = pl.multiple_of(jnp.clip(band * rows - SUB, 0, n * rows - size), SUB)
     per = size // pieces
@@ -132,7 +137,7 @@
 
 
 def lane_windows(terms, out):
-    arrays, _, rows, width = terms.shape
+    _, rows, width = terms.shape
     blocks = width // LANES
     size = LANES * (2 if blocks % 2 == 0 else 1)
     source = lax.broadcasted_iota(jnp.int32, (size, size), 0)
@@ -147,8 +152,7 @@
 
     def times(starts, wide, weights):
         left = [
-            jnp.concatenate([terms[a, t, :, start : start + wide] for t in range(3)], axis=1)
-            for a in range(arrays)
+            jnp.concatenate([terms[t, :, start : start + wide] for t in range(3)], axis=1)
             for start in starts
         ]
         got = jnp.dot(
@@ -156,17 +160,16 @@
             jnp.concatenate([weights] * 3, axis=0),
             preferred_element_type=F32,
         )
-        for i in range(len(left)):
-            yield divmod(i, len(starts)), got[i * rows : (i + 1) * rows]
+        return [got[i * rows : (i + 1) * rows] for i in range(len(left))]
 
     starts = list(range(0, width, size))
-    for (a, place), part in times(starts, size, inside):
-        out[a, :, starts[place] : starts[place] + size] = part
+    for start, part in zip(starts, times(starts, size, inside)):
+        out[:, start : start + size] = part
     starts = [start - LANES for start in starts[1:]]
     if starts:
-        for (a, place), part in times(starts, 2 * LANES, across):
-            at = slice(starts[place], starts[place] + 2 * LANES)
-            out[a, :, at] = out[a, :, at] + part
+        for start, part in zip(starts, times(starts, 2 * LANES, across)):
+            at = slice(start, start + 2 * LANES)
+            out[:, at] = out[:, at] + part
 
 
 def moving_kernel(n, rows, width, *refs):
@@ -186,7 +189,7 @@
     inv = 1.0 / float((2 * RADIUS + 1) ** 2)
     for terms in (sums, squares):
         clear_ends(terms)
-    for place, k in enumerate(hops(n) + [0]):
+    for place, k in enumerate(hops(n, MOVING_ORDER) + [0]):
         block = blocks[place]
         source = lax.rem(me - k + n, n)
         for y in range(0, deep, 2 * SUB):
@@ -215,8 +218,6 @@
                 shifted[block, c + REACH, y : y + SUB, :] = turned[
                     :, block * LANES : (block + 1) * LANES
                 ]
-    for copy in copies:
-        copy.wait()
     span = 2 * REACH + 2
 
     def unit(s, y0):
@@ -254,55 +255,74 @@
         linear[y0 : y0 + SUB, at] = cf * across + rf * (bottom_left - top_left)
         square[y0 : y0 + SUB, at] = (rf * cf) * ((bottom_right - bottom_left) - across)
 
+    for copy in copies:
+        copy.wait()
     for s in range(n):
         for g in range(rows // SUB):
             unit(s, g * SUB)
 
 
-def final_kernel(n, rows, width, chunks, *refs):
-    fixed, moving = refs[: n - 1], refs[n - 1 : 2 * n - 2]
-    base, linear, square, msum, mvar, own, out = refs[2 * n - 2 : 2 * n + 5]
-    summed, triple, terms, windows, products, obuf, sem = refs[2 * n + 5 :]
+def final_kernel(n, rows, width, *refs):
+    per = rows // STEPS
+    sem = refs[-1]
+
+    def result(step):
+        at = pl.ds(pl.multiple_of(step * per, SUB), per)
+        obuf, out = refs[-2], refs[2 * n + 4]
+        return pltpu.make_async_copy(obuf.at[at, :], out.at[at, :], sem.at[step])
+
+    def one(step, carry):
+        final_rows(n, per, width, pl.multiple_of(step * per, SUB), refs)
+        result(step).start()
+        return carry
+
+    lax.fori_loop(0, STEPS, one, 0)
+    for step in range(STEPS):
+        result(step).wait()
+
+
+def final_rows(n, rows, width, start, refs):
+    deep = pl.ds(start, rows + 2 * HALO)
+    here = pl.ds(start, rows)
+    fixed = [ref.at[deep, :] for ref in refs[: n - 1]]
+    moving = [ref.at[deep, :] for ref in refs[n - 1 : 2 * n - 2]]
+    base, linear, square, msum, mvar = [ref.at[here, :] for ref in refs[2 * n - 2 : 2 * n + 3]]
+    own = refs[2 * n + 3].at[:, here, :]
+    summed, triple, square_terms, cross_terms, windows, products, obuf = refs[2 * n + 5 : -1]
+    obuf = obuf.at[here, :]
     me = lax.axis_index("tile")
     inv = 1.0 / float((2 * RADIUS + 1) ** 2)
     extent = width + LANES
     summed[:, width:] = jnp.zeros((rows, LANES), F32)
-
-    def keep(source, totals):
-        at = pl.ds(pl.multiple_of(source * LANES, LANES), LANES)
-        for y in range(0, rows, 2 * SUB):
-            summed[y : y + 2 * SUB, at] = totals[0](y, 2 * SUB)
-            for which in range(2):
-                for t, part in enumerate(split(totals[1 + which](y, 2 * SUB))):
-                    terms[which, t, y : y + 2 * SUB, at] = part
-
-    keep(me, [lambda y, size, w=w: own[w, y : y + size, :] for w in range(3)])
-    for place, k in enumerate(hops(n)):
-        keep(
-            lax.rem(me - k + n, n),
-            fixed_row_sums(fixed[place], moving[place], products.at[place], rows),
-        )
-    lane_windows(terms, windows)
+    blocks = [(me, [lambda y, size, w=w: own[w, y : y + size, :] for w in range(3)])]
+    for place, k in enumerate(hops(n, FIXED_ORDER)):
+        totals = fixed_row_sums(fixed[place], moving[place], products.at[place], rows)
+        blocks.append((lax.rem(me - k + n, n), totals))
+
+    def places():
+        for source, totals in blocks:
+            yield pl.ds(pl.multiple_of(source * LANES, LANES), LANES), totals
+
+    for at, totals in places():
+        for y in range(0, rows, SUB):
+            summed[y : y + SUB, at] = totals[0](y, SUB)
     for y in range(0, rows, SUB):
         x = summed[y : y + SUB, :]
         triple[y : y + SUB, :] = x + pltpu.roll(x, 1, 1) + pltpu.roll(x, extent - 1, 1)
-    per = rows // chunks
-    copies = []
-    for chunk in range(chunks):
-        for y in range(chunk * per, (chunk + 1) * per, SUB):
-            at = slice(y, y + SUB)
-            x = triple[at, :]
-            fsum = (x + pltpu.roll(x, 3, 1) + pltpu.roll(x, extent - 3, 1))[:, :width]
-            fvar = windows[0, at, :] - fsum * fsum * inv
-            cov = windows[1, at, :] - fsum * msum[at, :] * inv
-            conf = 0.5 + 0.5 * (cov * lax.rsqrt(fvar * mvar[at, :] + 0.001))
-            obuf[at, :] = base[at, :] + conf * (linear[at, :] + conf * square[at, :])
-        span = pl.ds(chunk * per, per)
-        copy = pltpu.make_async_copy(obuf.at[span, :], out.at[span, :], sem.at[chunk])
-        copy.start()
-        copies.append(copy)
-    for copy in copies:
-        copy.wait()
+    for which, terms in enumerate((square_terms, cross_terms)):
+        for at, totals in places():
+            for y in range(0, rows, 2 * SUB):
+                for t, part in enumerate(split(totals[1 + which](y, 2 * SUB))):
+                    terms[t, y : y + 2 * SUB, at] = part
+        lane_windows(terms, windows.at[which])
+    for y in range(0, rows, SUB):
+        at = slice(y, y + SUB)
+        x = triple[at, :]
+        fsum = (x + pltpu.roll(x, 3, 1) + pltpu.roll(x, extent - 3, 1))[:, :width]
+        fvar = windows[0, at, :] - fsum * fsum * inv
+        cov = windows[1, at, :] - fsum * msum[at, :] * inv
+        conf = 0.5 + 0.5 * (cov * lax.rsqrt(fvar * mvar[at, :] + 0.001))
+        obuf[at, :] = base[at, :] + conf * (linear[at, :] + conf * square[at, :])
 
 
 VMEM = pl.BlockSpec(memory_space=pltpu.VMEM)
@@ -328,7 +348,7 @@
     band = held((deep, strip[1]))
     plane = held((rows, width))
     params = pltpu.CompilerParams(vmem_limit_bytes=ROOM)
-    pieces = 3
+    pieces = PIECES
     first = pl.pallas_call(
         functools.partial(first_kernel, n, rows, pieces),
         out_shape=band,
@@ -341,7 +361,7 @@
         compiler_params=params,
         name="first",
     )(far(moving))
-    order = hops(n)
+    order, later = hops(n, MOVING_ORDER), hops(n, FIXED_ORDER)
 
     def pack(image, shifts):
         return pl.pallas_call(
@@ -353,15 +373,18 @@
             name="pack",
         )(near(image))
 
-    def send(blocks):
-        got = [
-            lax.ppermute(block, "tile", [(i, (i + k) % n) for i in range(n)])
-            for block, k in zip(blocks, order)
-        ]
-        return got + [blocks[-1]]
-
-    moved = send([first, *pack(moving, order[1:] + [0])])
-    fixes = send(pack(fixed, order + [0]))
+    blocks = {("m", order[0]): first}
+    blocks.update(zip([("m", k) for k in order[1:] + [0]], pack(moving, order[1:] + [0])))
+    blocks.update(zip([("f", k) for k in later + [0]], pack(fixed, later + [0])))
+    turns = [("m", k) for k in order] + [("f", k) for k in later]
+    got = {
+        (image, k): lax.ppermute(
+            blocks[image, k], "tile", [(i, (i + k) % n) for i in range(n)]
+        )
+        for image, k in turns
+    }
+    moved = [got["m", k] for k in order] + [blocks["m", 0]]
+    fixes = [got["f", k] for k in later] + [blocks["f", 0]]
     parts = pl.pallas_call(
         functools.partial(moving_kernel, n, rows, width),
         out_shape=[plane] * 5 + [held((3, rows, strip[1]))],
@@ -385,24 +408,25 @@
         ),
         name="moving_part",
     )(*map(near, (*moved, fixes[-1])), far(offsets), far(fractions))
-    chunks = 4
+    per = rows // STEPS
     return pl.pallas_call(
-        functools.partial(final_kernel, n, rows, width, chunks),
+        functools.partial(final_kernel, n, rows, width),
         out_shape=jax.ShapeDtypeStruct((rows, width), F32),
         in_specs=[VMEM] * (2 * n + 4),
         out_specs=ANY,
         scratch_shapes=[
-            pltpu.VMEM((rows, width + LANES), F32),
-            pltpu.VMEM((rows, width + LANES), F32),
-            pltpu.VMEM((2, 3, rows, width), BF16),
-            pltpu.VMEM((2, rows, width), F32),
-            pltpu.VMEM((n - 1, 5, deep, LANES), F32),
+            pltpu.VMEM((per, width + LANES), F32),
+            pltpu.VMEM((per, width + LANES), F32),
+            pltpu.VMEM((3, per, width), BF16),
+            pltpu.VMEM((3, per, width), BF16),
+            pltpu.VMEM((2, per, width), F32),
+            pltpu.VMEM((n - 1, 5, per + 2 * HALO, LANES), F32),
             pltpu.VMEM((rows, width), F32),
-            pltpu.SemaphoreType.DMA((chunks,)),
+            pltpu.SemaphoreType.DMA((STEPS,)),
         ],
         compiler_params=params,
         name="final_part",
-    )(*map(near, (*fixes[:-1], *moved[:-1], *parts)))
+    )(*map(near, (*fixes[:-1], *(moved[order.index(k)] for k in later), *parts)))
 
 
 def solution(mesh):

time: 18.5 us -> 18.6 us (level)
  no operation moved by 1% of the time
where the time goes in v5:
time: 18.6 us; the launch traced here: 18.4 us
  starting transfers between devices  12 us (65%)
  Pallas kernels  5.64 us (30%)
  waiting for transfers between devices  0.78 us (4%)
    ppermute x6, starting transfers between devices, on_device(): lax.ppermute(blocks[image, k], 'tile', [(i, (i + k) % n) for i in range(n)])  12 us
    pallas_call x1, Pallas kernels, on_device(): pl.pallas_call(functools.partial(moving_kernel, n, rows, width), out_shap...  3.01 us
    pallas_call x1, Pallas kernels, on_device(): pl.pallas_call(functools.partial(final_kernel, n, rows, width), out_shape...  1.73 us
    pallas_call x1, Pallas kernels, on_device(): pl.pallas_call(functools.partial(first_kernel, n, rows, pieces), out_shap...  0.86 us
    ppermute x6, waiting for transfers between devices, on_device(): lax.ppermute(blocks[image, k], 'tile', [(i, (i + k) % n) for i in range(n)])  0.78 us
  transfers between devices with their start and end apart: 6, of which 2 were waited for; matrix products, arithmetic and copies ran while one was open for 0% of the time, Pallas kernels for 17%

profile of v5, /device:TPU:0, one launch (start us, length us, event | category | flops | bytes accessed | tf_op | source)
XLA Modules:
  0.0 18.4 jit_solution(9993925734752312754)
XLA Ops:
  0.0 0.0 copy-start
  0.0 0.0 copy-start.1
  0.0 0.9 %first.1 = f32[136,128]{1,0:T(8,128)S(1)} custom-call(f32[512,128]{1,0:T(8,128)} %strip.3), custom_call_target="tpu_custom_call" | custom-call | tf_op jit(solution)/shard_map/first/pallas_call | solution.py:352
  0.9 4.1 %collective-permute-start.3 = (f32[136,128]{1,0:T(8,128)S(1)}, f32[136,128]{1,0:T(8,128)S(1)}, u32[]{:S(2)}, u32[]{:S(2)}) collective-permute-start(f32[136,128]{1,0:T(8,128)S(1)} %first.1), channel_id=1, source_target_pairs={{0,2},{1,3},{2,0},{3,1},{4,6},{5,7},{6,4},{7,5},{8,10},{9,11},{10,... | collective-permute-start | bytes 208904 | tf_op jit(solution)/shard_map/ppermute | solution.py:381
  5.0 0.0 copy-done
  5.0 1.6 %collective-permute-start.4 = (f32[136,128]{1,0:T(8,128)S(1)}, f32[136,128]{1,0:T(8,128)S(1)}, u32[]{:S(2)}, u32[]{:S(2)}) collective-permute-start(f32[136,128]{1,0:T(8,128)S(1)} %get-tuple-element.21), channel_id=1, source_target_pairs={{0,1},{1,2},{2,3},{3,0},{4,5},{5,6},{6,7},{7,4},{8,9},{9,10},{10,1... | collective-permute-start | bytes 208904 | tf_op jit(solution)/shard_map/ppermute | solution.py:381
  6.7 2.2 %collective-permute-start.5 = (f32[136,128]{1,0:T(8,128)S(1)}, f32[136,128]{1,0:T(8,128)S(1)}, u32[]{:S(2)}, u32[]{:S(2)}) collective-permute-start(f32[136,128]{1,0:T(8,128)S(1)} %get-tuple-element.22), channel_id=1, source_target_pairs={{0,3},{1,0},{2,1},{3,2},{4,7},{5,4},{6,5},{7,6},{8,11},{9,8},{10,9... | collective-permute-start | bytes 208904 | tf_op jit(solution)/shard_map/ppermute | solution.py:381
  8.9 0.0 copy-done.1
  8.9 0.1 collective-permute-start
  9.0 0.6 %collective-permute-start.1 = (f32[136,128]{1,0:T(8,128)S(1)}, f32[136,128]{1,0:T(8,128)S(1)}, u32[]{:S(2)}, u32[]{:S(2)}) collective-permute-start(f32[136,128]{1,0:T(8,128)S(1)} %get-tuple-element.19), channel_id=1, source_target_pairs={{0,1},{1,2},{2,3},{3,0},{4,5},{5,6},{6,7},{7,4},{8,9},{9,10},{10,1... | collective-permute-start | bytes 208904 | tf_op jit(solution)/shard_map/ppermute | solution.py:381
  9.6 0.0 collective-permute-done.3.refs_0_.refs_3_
  9.6 3.3 %collective-permute-start.2 = (f32[136,128]{1,0:T(8,128)S(1)}, f32[136,128]{1,0:T(8,128)S(1)}, u32[]{:S(2)}, u32[]{:S(2)}) collective-permute-start(f32[136,128]{1,0:T(8,128)S(1)} %get-tuple-element.20), channel_id=1, source_target_pairs={{0,3},{1,0},{2,1},{3,2},{4,7},{5,4},{6,5},{7,6},{8,11},{9,8},{10,9... | collective-permute-start | bytes 208904 | tf_op jit(solution)/shard_map/ppermute | solution.py:381
  12.9 0.0 collective-permute-done.4.refs_1_.refs_4_
  12.9 0.0 collective-permute-done.5.refs_2_.refs_5_
  12.9 3.0 %moving_part.1 = (f32[128,512]{1,0:T(8,128)S(1)}, f32[128,512]{1,0:T(8,128)S(1)}, f32[128,512]{1,0:T(8,128)S(1)}, f32[128,512]{1,0:T(8,128)S(1)}, f32[128,512]{1,0:T(8,128)S(1)}, /*index=5*/f32[3,128,128]{2,1,0:T(8,128)S(1)}) custom-call(f32[136,128]{1,0:T(8,128)S(1)} %collective-permute-done.3.refs_0_.refs_3_, ...), custom_call_target="tpu_custom_call" | custom-call | flops 13107200 | bytes 1048576 | tf_op jit(solution)/shard_map/moving_part/pallas_call | solution.py:388
  15.9 0.6 %collective-permute-done.refs_0_ = f32[136,128]{1,0:T(8,128)S(1)} collective-permute-done((f32[136,128]{1,0:T(8,128)S(1)}, f32[136,128]{1,0:T(8,128)S(1)}, u32[]{:S(2)}, u32[]{:S(2)}) %collective-permute-start) | collective-permute-done | bytes 69664 | tf_op jit(solution)/shard_map/ppermute | solution.py:381
  16.5 0.0 collective-permute-done.1.refs_1_
  16.5 0.2 collective-permute-done.2.refs_2_
  16.7 1.7 %final_part.1 = f32[128,512]{1,0:T(8,128)} custom-call(f32[136,128]{1,0:T(8,128)S(1)} %collective-permute-done.refs_0_, f32[136,128]{1,0:T(8,128)S(1)} %collective-permute-done.1.refs_1_, f32[136,128]{1,0:T(8,128)S(1)} %collective-permute-done.2.refs_2_, f32[136,128]{1,0:T(8,128)S(1)} %collective-permute-done.3.refs_0_.refs_3_, ...), custom_call_target="tpu_custom_call" | custom-call | tf_op jit(solution)/shard_map/final_part/pallas_call | solution.py:412
  (2 shorter events, 0.0 us)
Async XLA Ops:
  0.0 5.0 %copy-start = (f32[512,128]{1,0:T(8,128)S(1)}, f32[512,128]{1,0:T(8,128)}, u32[]{:S(2)}) copy-start(f32[512,128]{1,0:T(8,128)} %strip.3) | copy-start | bytes 786436
  0.0 8.9 %copy-start.1 = (f32[512,128]{1,0:T(8,128)S(1)}, f32[512,128]{1,0:T(8,128)}, u32[]{:S(2)}) copy-start(f32[512,128]{1,0:T(8,128)} %strip.2) | copy-start | bytes 786436
  0.9 8.7 %collective-permute-start.3 = (f32[136,128]{1,0:T(8,128)S(1)}, f32[136,128]{1,0:T(8,128)S(1)}, u32[]{:S(2)}, u32[]{:S(2)}) collective-permute-start(f32[136,128]{1,0:T(8,128)S(1)} %first.1), channel_id=1, source_target_pairs={{0,2},{1,3},{2,0},{3,1},{4,6},{5,7},{6,4},{7,5},{8,10},{9,11},{10,... | collective-permute-start | bytes 208904 | tf_op jit(solution)/shard_map/ppermute | solution.py:381
  5.0 7.9 %collective-permute-start.4 = (f32[136,128]{1,0:T(8,128)S(1)}, f32[136,128]{1,0:T(8,128)S(1)}, u32[]{:S(2)}, u32[]{:S(2)}) collective-permute-start(f32[136,128]{1,0:T(8,128)S(1)} %get-tuple-element.21), channel_id=1, source_target_pairs={{0,1},{1,2},{2,3},{3,0},{4,5},{5,6},{6,7},{7,4},{8,9},{9,10},{10,1... | collective-permute-start | bytes 208904 | tf_op jit(solution)/shard_map/ppermute | solution.py:381
  6.7 6.2 %collective-permute-start.5 = (f32[136,128]{1,0:T(8,128)S(1)}, f32[136,128]{1,0:T(8,128)S(1)}, u32[]{:S(2)}, u32[]{:S(2)}) collective-permute-start(f32[136,128]{1,0:T(8,128)S(1)} %get-tuple-element.22), channel_id=1, source_target_pairs={{0,3},{1,0},{2,1},{3,2},{4,7},{5,4},{6,5},{7,6},{8,11},{9,8},{10,9... | collective-permute-start | bytes 208904 | tf_op jit(solution)/shard_map/ppermute | solution.py:381
  8.9 7.6 %collective-permute-start = (f32[136,128]{1,0:T(8,128)S(1)}, f32[136,128]{1,0:T(8,128)S(1)}, u32[]{:S(2)}, u32[]{:S(2)}) collective-permute-start(f32[136,128]{1,0:T(8,128)S(1)} %get-tuple-element.18), channel_id=1, source_target_pairs={{0,2},{1,3},{2,0},{3,1},{4,6},{5,7},{6,4},{7,5},{8,10},{9,11},{10,... | collective-permute-start | bytes 208904 | tf_op jit(solution)/shard_map/ppermute | solution.py:381
  9.0 7.5 %collective-permute-start.1 = (f32[136,128]{1,0:T(8,128)S(1)}, f32[136,128]{1,0:T(8,128)S(1)}, u32[]{:S(2)}, u32[]{:S(2)}) collective-permute-start(f32[136,128]{1,0:T(8,128)S(1)} %get-tuple-element.19), channel_id=1, source_target_pairs={{0,1},{1,2},{2,3},{3,0},{4,5},{5,6},{6,7},{7,4},{8,9},{9,10},{10,1... | collective-permute-start | bytes 208904 | tf_op jit(solution)/shard_map/ppermute | solution.py:381
  9.6 7.1 %collective-permute-start.2 = (f32[136,128]{1,0:T(8,128)S(1)}, f32[136,128]{1,0:T(8,128)S(1)}, u32[]{:S(2)}, u32[]{:S(2)}) collective-permute-start(f32[136,128]{1,0:T(8,128)S(1)} %get-tuple-element.20), channel_id=1, source_target_pairs={{0,3},{1,0},{2,1},{3,2},{4,7},{5,4},{6,5},{7,6},{8,11},{9,8},{10,9... | collective-permute-start | bytes 208904 | tf_op jit(solution)/shard_map/ppermute | solution.py:381

commit v6 on v5

--- a/solution.py
+++ b/solution.py
@@ -18,7 +18,7 @@
 
 
 PIECES = 3
-STEPS = 2
+STEPS = 1
 MOVING_ORDER = (2, 1, 3)
 FIXED_ORDER = (2, 1, 3)
 

time: 18.6 us -> 18.6 us (level)
  no operation moved by 1% of the time
where the time goes in v6:
time: 18.6 us; the launch traced here: 18.4 us
  starting transfers between devices  12 us (65%)
  Pallas kernels  5.63 us (30%)
  waiting for transfers between devices  0.78 us (4%)
    ppermute x6, starting transfers between devices, on_device(): lax.ppermute(blocks[image, k], 'tile', [(i, (i + k) % n) for i in range(n)])  12 us
    pallas_call x1, Pallas kernels, on_device(): pl.pallas_call(functools.partial(moving_kernel, n, rows, width), out_shap...  3.01 us
    pallas_call x1, Pallas kernels, on_device(): pl.pallas_call(functools.partial(final_kernel, n, rows, width), out_shape...  1.72 us
    pallas_call x1, Pallas kernels, on_device(): pl.pallas_call(functools.partial(first_kernel, n, rows, pieces), out_shap...  0.86 us
    ppermute x6, waiting for transfers between devices, on_device(): lax.ppermute(blocks[image, k], 'tile', [(i, (i + k) % n) for i in range(n)])  0.78 us
  transfers between devices with their start and end apart: 6, of which 2 were waited for; matrix products, arithmetic and copies ran while one was open for 0% of the time, Pallas kernels for 17%

profile of v6, /device:TPU:0, one launch (start us, length us, event | category | flops | bytes accessed | tf_op | source)
XLA Modules:
  0.0 18.4 jit_solution(18045679119419024829)
XLA Ops:
  0.0 0.0 copy-start
  0.0 0.0 copy-start.1
  0.0 0.9 %first.1 = f32[136,128]{1,0:T(8,128)S(1)} custom-call(f32[512,128]{1,0:T(8,128)} %strip.3), custom_call_target="tpu_custom_call" | custom-call | tf_op jit(solution)/shard_map/first/pallas_call | solution.py:352
  0.9 4.1 %collective-permute-start.3 = (f32[136,128]{1,0:T(8,128)S(1)}, f32[136,128]{1,0:T(8,128)S(1)}, u32[]{:S(2)}, u32[]{:S(2)}) collective-permute-start(f32[136,128]{1,0:T(8,128)S(1)} %first.1), channel_id=1, source_target_pairs={{0,2},{1,3},{2,0},{3,1},{4,6},{5,7},{6,4},{7,5},{8,10},{9,11},{10,... | collective-permute-start | bytes 208904 | tf_op jit(solution)/shard_map/ppermute | solution.py:381
  5.0 0.0 copy-done
  5.0 1.6 %collective-permute-start.4 = (f32[136,128]{1,0:T(8,128)S(1)}, f32[136,128]{1,0:T(8,128)S(1)}, u32[]{:S(2)}, u32[]{:S(2)}) collective-permute-start(f32[136,128]{1,0:T(8,128)S(1)} %get-tuple-element.21), channel_id=1, source_target_pairs={{0,1},{1,2},{2,3},{3,0},{4,5},{5,6},{6,7},{7,4},{8,9},{9,10},{10,1... | collective-permute-start | bytes 208904 | tf_op jit(solution)/shard_map/ppermute | solution.py:381
  6.7 2.2 %collective-permute-start.5 = (f32[136,128]{1,0:T(8,128)S(1)}, f32[136,128]{1,0:T(8,128)S(1)}, u32[]{:S(2)}, u32[]{:S(2)}) collective-permute-start(f32[136,128]{1,0:T(8,128)S(1)} %get-tuple-element.22), channel_id=1, source_target_pairs={{0,3},{1,0},{2,1},{3,2},{4,7},{5,4},{6,5},{7,6},{8,11},{9,8},{10,9... | collective-permute-start | bytes 208904 | tf_op jit(solution)/shard_map/ppermute | solution.py:381
  8.9 0.0 copy-done.1
  8.9 0.1 collective-permute-start
  9.0 0.6 %collective-permute-start.1 = (f32[136,128]{1,0:T(8,128)S(1)}, f32[136,128]{1,0:T(8,128)S(1)}, u32[]{:S(2)}, u32[]{:S(2)}) collective-permute-start(f32[136,128]{1,0:T(8,128)S(1)} %get-tuple-element.19), channel_id=1, source_target_pairs={{0,1},{1,2},{2,3},{3,0},{4,5},{5,6},{6,7},{7,4},{8,9},{9,10},{10,1... | collective-permute-start | bytes 208904 | tf_op jit(solution)/shard_map/ppermute | solution.py:381
  9.6 0.0 collective-permute-done.3.refs_0_.refs_3_
  9.6 3.3 %collective-permute-start.2 = (f32[136,128]{1,0:T(8,128)S(1)}, f32[136,128]{1,0:T(8,128)S(1)}, u32[]{:S(2)}, u32[]{:S(2)}) collective-permute-start(f32[136,128]{1,0:T(8,128)S(1)} %get-tuple-element.20), channel_id=1, source_target_pairs={{0,3},{1,0},{2,1},{3,2},{4,7},{5,4},{6,5},{7,6},{8,11},{9,8},{10,9... | collective-permute-start | bytes 208904 | tf_op jit(solution)/shard_map/ppermute | solution.py:381
  12.9 0.0 collective-permute-done.4.refs_1_.refs_4_
  12.9 0.0 collective-permute-done.5.refs_2_.refs_5_
  12.9 3.0 %moving_part.1 = (f32[128,512]{1,0:T(8,128)S(1)}, f32[128,512]{1,0:T(8,128)S(1)}, f32[128,512]{1,0:T(8,128)S(1)}, f32[128,512]{1,0:T(8,128)S(1)}, f32[128,512]{1,0:T(8,128)S(1)}, /*index=5*/f32[3,128,128]{2,1,0:T(8,128)S(1)}) custom-call(f32[136,128]{1,0:T(8,128)S(1)} %collective-permute-done.3.refs_0_.refs_3_, ...), custom_call_target="tpu_custom_call" | custom-call | flops 13107200 | bytes 1048576 | tf_op jit(solution)/shard_map/moving_part/pallas_call | solution.py:388
  15.9 0.6 %collective-permute-done.refs_0_ = f32[136,128]{1,0:T(8,128)S(1)} collective-permute-done((f32[136,128]{1,0:T(8,128)S(1)}, f32[136,128]{1,0:T(8,128)S(1)}, u32[]{:S(2)}, u32[]{:S(2)}) %collective-permute-start) | collective-permute-done | bytes 69664 | tf_op jit(solution)/shard_map/ppermute | solution.py:381
  16.5 0.0 collective-permute-done.1.refs_1_
  16.5 0.2 collective-permute-done.2.refs_2_
  16.7 1.7 %final_part.1 = f32[128,512]{1,0:T(8,128)} custom-call(f32[136,128]{1,0:T(8,128)S(1)} %collective-permute-done.refs_0_, f32[136,128]{1,0:T(8,128)S(1)} %collective-permute-done.1.refs_1_, f32[136,128]{1,0:T(8,128)S(1)} %collective-permute-done.2.refs_2_, f32[136,128]{1,0:T(8,128)S(1)} %collective-permute-done.3.refs_0_.refs_3_, ...), custom_call_target="tpu_custom_call" | custom-call | tf_op jit(solution)/shard_map/final_part/pallas_call | solution.py:412
  (2 shorter events, 0.0 us)
Async XLA Ops:
  0.0 5.0 %copy-start = (f32[512,128]{1,0:T(8,128)S(1)}, f32[512,128]{1,0:T(8,128)}, u32[]{:S(2)}) copy-start(f32[512,128]{1,0:T(8,128)} %strip.3) | copy-start | bytes 786436
  0.0 8.9 %copy-start.1 = (f32[512,128]{1,0:T(8,128)S(1)}, f32[512,128]{1,0:T(8,128)}, u32[]{:S(2)}) copy-start(f32[512,128]{1,0:T(8,128)} %strip.2) | copy-start | bytes 786436
  0.9 8.7 %collective-permute-start.3 = (f32[136,128]{1,0:T(8,128)S(1)}, f32[136,128]{1,0:T(8,128)S(1)}, u32[]{:S(2)}, u32[]{:S(2)}) collective-permute-start(f32[136,128]{1,0:T(8,128)S(1)} %first.1), channel_id=1, source_target_pairs={{0,2},{1,3},{2,0},{3,1},{4,6},{5,7},{6,4},{7,5},{8,10},{9,11},{10,... | collective-permute-start | bytes 208904 | tf_op jit(solution)/shard_map/ppermute | solution.py:381
  5.0 7.9 %collective-permute-start.4 = (f32[136,128]{1,0:T(8,128)S(1)}, f32[136,128]{1,0:T(8,128)S(1)}, u32[]{:S(2)}, u32[]{:S(2)}) collective-permute-start(f32[136,128]{1,0:T(8,128)S(1)} %get-tuple-element.21), channel_id=1, source_target_pairs={{0,1},{1,2},{2,3},{3,0},{4,5},{5,6},{6,7},{7,4},{8,9},{9,10},{10,1... | collective-permute-start | bytes 208904 | tf_op jit(solution)/shard_map/ppermute | solution.py:381
  6.7 6.2 %collective-permute-start.5 = (f32[136,128]{1,0:T(8,128)S(1)}, f32[136,128]{1,0:T(8,128)S(1)}, u32[]{:S(2)}, u32[]{:S(2)}) collective-permute-start(f32[136,128]{1,0:T(8,128)S(1)} %get-tuple-element.22), channel_id=1, source_target_pairs={{0,3},{1,0},{2,1},{3,2},{4,7},{5,4},{6,5},{7,6},{8,11},{9,8},{10,9... | collective-permute-start | bytes 208904 | tf_op jit(solution)/shard_map/ppermute | solution.py:381
  8.9 7.6 %collective-permute-start = (f32[136,128]{1,0:T(8,128)S(1)}, f32[136,128]{1,0:T(8,128)S(1)}, u32[]{:S(2)}, u32[]{:S(2)}) collective-permute-start(f32[136,128]{1,0:T(8,128)S(1)} %get-tuple-element.18), channel_id=1, source_target_pairs={{0,2},{1,3},{2,0},{3,1},{4,6},{5,7},{6,4},{7,5},{8,10},{9,11},{10,... | collective-permute-start | bytes 208904 | tf_op jit(solution)/shard_map/ppermute | solution.py:381
  9.0 7.5 %collective-permute-start.1 = (f32[136,128]{1,0:T(8,128)S(1)}, f32[136,128]{1,0:T(8,128)S(1)}, u32[]{:S(2)}, u32[]{:S(2)}) collective-permute-start(f32[136,128]{1,0:T(8,128)S(1)} %get-tuple-element.19), channel_id=1, source_target_pairs={{0,1},{1,2},{2,3},{3,0},{4,5},{5,6},{6,7},{7,4},{8,9},{9,10},{10,1... | collective-permute-start | bytes 208904 | tf_op jit(solution)/shard_map/ppermute | solution.py:381
  9.6 7.1 %collective-permute-start.2 = (f32[136,128]{1,0:T(8,128)S(1)}, f32[136,128]{1,0:T(8,128)S(1)}, u32[]{:S(2)}, u32[]{:S(2)}) collective-permute-start(f32[136,128]{1,0:T(8,128)S(1)} %get-tuple-element.20), channel_id=1, source_target_pairs={{0,3},{1,0},{2,1},{3,2},{4,7},{5,4},{6,5},{7,6},{8,11},{9,8},{10,9... | collective-permute-start | bytes 208904 | tf_op jit(solution)/shard_map/ppermute | solution.py:381
